TPU v7x, 32 devices: a whole 2x2x4 slice. The times are simulated.
32 devices in a mesh: tm: 2 (over y), clip: 4 (over x, core), mp: 4 (over z).
Axes of the slice: x: 2, y: 2, z: 4, core: 2. Of those that a mesh axis runs over, the one named last changes fastest.
Arguments:
- tokens: bfloat16 [8, 16, 128, 1024], P('clip', 'tm', None, 'mp'), may hold values from -6 to 6
- cotangent: bfloat16 [8, 16, 128, 1024], P('clip', 'tm', None, 'mp'), may hold values from -6 to 6
- ratio: int32 [8], P('clip'), may hold values from 50 to 100
- priority: int32 [8, 16, 128], P('clip', 'tm'), may hold values from 0 to 99
- frame_order: int32 [8, 16], P('clip'), may hold values from 0 to 15, each once within a row
- mask_embed: bfloat16 [1024], P('mp'), may hold values from -6 to 6
- gains: bfloat16 [3, 1024], P(None, 'mp'), may hold values from 0.099609375 to 1.8984375
- qkv_space: bfloat16 [1024, 3, 1024], P(None, None, 'mp'), may hold values from -0.1875 to 0.1875
- out_space: bfloat16 [1024, 1024], P('mp'), may hold values from -0.75 to 0.75
- qkv_time: bfloat16 [1024, 3, 1024], P(None, None, 'mp'), may hold values from -0.1875 to 0.1875
- out_time: bfloat16 [1024, 1024], P('mp'), may hold values from -0.375 to 0.375
- w_in: bfloat16 [1024, 4096], P(None, 'mp'), may hold values from -0.1875 to 0.1875
- w_out: bfloat16 [4096, 1024], P('mp'), may hold values from -0.09375 to 0.09375
Outputs:
- block_out: bfloat16 [8, 16, 128, 1024], P('clip', 'tm', None, 'mp')
- grad_tokens: float32 [8, 16, 128, 1024], P('clip', 'tm', None, 'mp')
- grad_mask_embed: float32 [1024], P('mp')
- grad_gains: float32 [3, 1024], P(None, 'mp')
- grad_qkv_space: float32 [1024, 3, 1024], P(('tm', 'clip'), None, 'mp')
- grad_out_space: float32 [1024, 1024], P('mp', ('tm', 'clip'))
- grad_qkv_time: float32 [1024, 3, 1024], P(('tm', 'clip'), None, 'mp')
- grad_out_time: float32 [1024, 1024], P('mp', ('tm', 'clip'))
- grad_w_in: float32 [1024, 4096], P(('tm', 'clip'), 'mp')
- grad_w_out: float32 [4096, 1024], P('mp', ('tm', 'clip'))
Inputs may be any that keep to these rules, and one draw needn't show every extreme that they name: Each row of frame_order holds each of 0 to 15 once.
All inputs are finite; a program needn't handle non-finite values.
Results may differ from a plain program's by a relative error of at most 0.02.
Values may be sent and summed in bfloat16 or wider, within the bound.
A program may use at most 192 MiB of HBM per device.

v0:
```python
import functools
import math

import jax
import jax.numpy as jnp
from jax import lax
from jax.experimental import pallas as pl
from jax.experimental.pallas import tpu as pltpu
from jax.sharding import PartitionSpec as P

HEAD_DIM = 64
MICRO = 2


eps_norm = 1e-05


def gelu_tanh(values):
    return jax.nn.gelu(values, approximate=True)


def norm_forward_pass(residual_stream, gain_coefficients, complete_width):
    reduced_totals = lax.psum(
        (jnp.sum(residual_stream, axis=-1), jnp.sum(residual_stream * residual_stream, axis=-1)),
        "mp",
    )
    centered_rows = reduced_totals[0] / complete_width
    spread = reduced_totals[1] / complete_width - centered_rows * centered_rows
    inverse_scale = lax.rsqrt(spread + eps_norm)
    standardized_rows = (residual_stream - centered_rows[:, None]) * inverse_scale[:, None]
    shard_rows = (standardized_rows * gain_coefficients).astype(jnp.bfloat16)
    normalized_rows = lax.all_gather(shard_rows, "mp", axis=1, tiled=True)
    return (normalized_rows, standardized_rows, inverse_scale)


def norm_reverse_pass(
    normalized_gradient, standardized_rows, inverse_scale, gain_coefficients, complete_width
):
    gain_gradient = jnp.sum(normalized_gradient * standardized_rows, axis=0)
    standardized_gradient = normalized_gradient * gain_coefficients
    reduced_totals = lax.psum(
        (
            jnp.sum(standardized_gradient, axis=-1),
            jnp.sum(standardized_gradient * standardized_rows, axis=-1),
        ),
        "mp",
    )
    grad_resid = (
        standardized_gradient
        - reduced_totals[0][:, None] / complete_width
        - standardized_rows * (reduced_totals[1][:, None] / complete_width)
    ) * inverse_scale[:, None]
    return (grad_resid, gain_gradient)


def sum_features(grad_full):
    return lax.psum_scatter(
        grad_full.astype(jnp.bfloat16), "mp", scatter_dimension=1, tiled=True
    ).astype(jnp.float32)


def branch_out(hidden, weight):
    partial_rows = jnp.dot(hidden, weight, preferred_element_type=jnp.float32)
    return lax.psum_scatter(partial_rows, "mp", scatter_dimension=1, tiled=True)


def branch_back(grad_resid, hidden, weight):
    grad_rows = lax.all_gather(grad_resid.astype(jnp.bfloat16), "mp", axis=1, tiled=True)
    weight_grad = jnp.einsum("rk,rd->kd", hidden, grad_rows, preferred_element_type=jnp.float32)
    grad_hidden = jnp.einsum("rd,kd->rk", grad_rows, weight, preferred_element_type=jnp.float32)
    return (grad_hidden, weight_grad)


def qkv_back(normalized_rows, grad_joined, weight):
    weight_grad = jnp.einsum(
        "rd,trk->dtk", normalized_rows, grad_joined, preferred_element_type=jnp.float32
    )
    grad_full = jnp.einsum("trk,dtk->rd", grad_joined, weight, preferred_element_type=jnp.float32)
    return (weight_grad, sum_features(grad_full))


def reduce_grads(local_grads, small_grads):
    reduced = (
        lax.psum_scatter(local_grads[0], ("tm", "clip"), scatter_dimension=0, tiled=True),
        lax.psum_scatter(local_grads[1], ("tm", "clip"), scatter_dimension=1, tiled=True),
        lax.psum_scatter(local_grads[2], ("tm", "clip"), scatter_dimension=0, tiled=True),
        lax.psum_scatter(local_grads[3], ("tm", "clip"), scatter_dimension=1, tiled=True),
        lax.psum_scatter(local_grads[4], ("tm", "clip"), scatter_dimension=0, tiled=True),
        lax.psum_scatter(local_grads[5], ("tm", "clip"), scatter_dimension=1, tiled=True),
    )
    reduced_small = lax.psum((small_grads[0], small_grads[1]), ("tm", "clip"))
    return (reduced, reduced_small)


def space_forward(normalized_rows, weight, frame_count, patches, heads_local, scale):
    joined = jnp.einsum(
        "rd,dtk->trk", normalized_rows, weight, preferred_element_type=jnp.float32
    ).astype(jnp.bfloat16)
    shape_heads = (frame_count, patches, heads_local, HEAD_DIM)
    scores = (
        jnp.einsum(
            "bshd,bthd->bhst",
            joined[0].reshape(shape_heads),
            joined[1].reshape(shape_heads),
            preferred_element_type=jnp.float32,
        )
        * scale
    )
    highest = jnp.max(scores, axis=-1, keepdims=True)
    exponent = jnp.exp(scores - highest)
    reduced_totals = jnp.sum(exponent, axis=-1, keepdims=True)
    log_total = highest + jnp.log(reduced_totals)
    attention = (exponent / reduced_totals).astype(jnp.bfloat16)
    mixed = jnp.einsum(
        "bhst,bthd->bshd",
        attention,
        joined[2].reshape(shape_heads),
        preferred_element_type=jnp.float32,
    )
    return (
        joined,
        log_total,
        mixed.astype(jnp.bfloat16).reshape(frame_count * patches, heads_local * HEAD_DIM),
    )


def space_backward(grad_mixed, joined, log_total, frame_count, patches, heads_local, scale):
    shape_heads = (frame_count, patches, heads_local, HEAD_DIM)
    queries = joined[0].reshape(shape_heads)
    key_rows = joined[1].reshape(shape_heads)
    values = joined[2].reshape(shape_heads)
    grad_out = grad_mixed.reshape(shape_heads)
    scores = (
        jnp.einsum("bshd,bthd->bhst", queries, key_rows, preferred_element_type=jnp.float32) * scale
    )
    attention = jnp.exp(scores - log_total)
    grad_values = jnp.einsum(
        "bhst,bshd->bthd",
        attention.astype(jnp.bfloat16),
        grad_out,
        preferred_element_type=jnp.float32,
    )
    grad_att = jnp.einsum("bshd,bthd->bhst", grad_out, values, preferred_element_type=jnp.float32)
    grad_scores = (
        attention * (grad_att - jnp.sum(attention * grad_att, axis=-1, keepdims=True))
    ).astype(jnp.bfloat16)
    grad_queries = (
        jnp.einsum("bhst,bthd->bshd", grad_scores, key_rows, preferred_element_type=jnp.float32)
        * scale
    )
    grad_keys = (
        jnp.einsum("bhst,bshd->bthd", grad_scores, queries, preferred_element_type=jnp.float32)
        * scale
    )
    row_count = frame_count * patches
    stacked = jnp.stack(
        [
            grad_queries.reshape(row_count, -1),
            grad_keys.reshape(row_count, -1),
            grad_values.reshape(row_count, -1),
        ]
    )
    return stacked.astype(jnp.bfloat16)


def time_scores(queries, keys_all, visible, scale):
    scores = (
        jnp.einsum("cfshd,cgshd->chfgs", queries, keys_all, preferred_element_type=jnp.float32)
        * scale
    )
    return jnp.where(visible, scores, -1e30)


def time_forward(queries, keys_all, values_all, visible, scale):
    scores = time_scores(queries, keys_all, visible, scale)
    highest = jnp.max(scores, axis=3, keepdims=True)
    exponent = jnp.exp(scores - highest)
    reduced_totals = jnp.sum(exponent, axis=3, keepdims=True)
    log_total = highest + jnp.log(reduced_totals)
    attention = (exponent / reduced_totals).astype(jnp.bfloat16)
    mixed = jnp.einsum(
        "chfgs,cgshd->cfshd", attention, values_all, preferred_element_type=jnp.float32
    )
    return (log_total, mixed.astype(jnp.bfloat16))


def time_backward(grad_mixed, queries, keys_all, values_all, visible, log_total, scale):
    grad_out = grad_mixed.reshape(queries.shape)
    scores = time_scores(queries, keys_all, visible, scale)
    attention = jnp.exp(scores - log_total)
    grad_values = jnp.einsum(
        "chfgs,cfshd->cgshd",
        attention.astype(jnp.bfloat16),
        grad_out,
        preferred_element_type=jnp.float32,
    )
    grad_att = jnp.einsum(
        "cfshd,cgshd->chfgs", grad_out, values_all, preferred_element_type=jnp.float32
    )
    grad_scores = (
        attention * (grad_att - jnp.sum(attention * grad_att, axis=3, keepdims=True))
    ).astype(jnp.bfloat16)
    grad_queries = (
        jnp.einsum("chfgs,cgshd->cfshd", grad_scores, keys_all, preferred_element_type=jnp.float32)
        * scale
    )
    grad_keys = (
        jnp.einsum("chfgs,cfshd->cgshd", grad_scores, queries, preferred_element_type=jnp.float32)
        * scale
    )
    return (grad_queries, grad_keys, grad_values)


def shards(
    tokens,
    cotangent,
    ratio,
    priority,
    frame_order,
    mask_embed,
    gains,
    qkv_space,
    out_space,
    qkv_time,
    out_time,
    w_in,
    w_out,
):
    scale = 1.0 / math.sqrt(HEAD_DIM)
    clips_local = tokens.shape[0] // MICRO
    frames_local = tokens.shape[1]
    patches = tokens.shape[2]
    cols_local = tokens.shape[3]
    frames_all = frame_order.shape[1]
    hidden_width = qkv_space.shape[0]
    joined_local = qkv_space.shape[2]
    heads_local = joined_local // HEAD_DIM
    row_count = clips_local * frames_local * patches
    gain_broadcast = gains.astype(jnp.float32)
    embed_row = mask_embed.astype(jnp.float32)
    first_frame = lax.axis_index("tm") * frames_local
    shape_local = (clips_local, frames_local, patches, joined_local)
    shape_heads = (clips_local, frames_local, patches, heads_local, HEAD_DIM)
    shape_all = (clips_local, frames_all, patches, heads_local, HEAD_DIM)
    outputs = []
    input_grads = []
    weight_total = None
    small_total = None
    for batch_index in range(MICRO):
        lower = batch_index * clips_local
        upper = lower + clips_local
        source = tokens[lower:upper].reshape(row_count, cols_local).astype(jnp.float32)
        upstream = cotangent[lower:upper].reshape(row_count, cols_local).astype(jnp.float32)
        masked = (priority[lower:upper] < ratio[lower:upper][:, None, None]).reshape(row_count)
        order_rows = frame_order[lower:upper]
        residual_stream0 = jnp.where(masked[:, None], embed_row[None, :], source)
        normalized_rows0, standardized_rows0, inverse_deviation0 = norm_forward_pass(
            residual_stream0, gain_broadcast[0], hidden_width
        )
        joined0, total0, mixed0 = space_forward(
            normalized_rows0, qkv_space, clips_local * frames_local, patches, heads_local, scale
        )
        residual_stream1 = residual_stream0 + branch_out(mixed0, out_space)
        normalized_rows1, standardized_rows1, inverse_deviation1 = norm_forward_pass(
            residual_stream1, gain_broadcast[1], hidden_width
        )
        joined1 = jnp.einsum(
            "rd,dtk->trk", normalized_rows1, qkv_time, preferred_element_type=jnp.float32
        ).astype(jnp.bfloat16)
        queries_local = joined1[0].reshape(shape_local)
        keys_local = joined1[1].reshape(shape_local)
        values_local = joined1[2].reshape(shape_local)
        keys_all, values_all = (
            lax.all_gather(keys_local, "tm", axis=1, tiled=True),
            lax.all_gather(values_local, "tm", axis=1, tiled=True),
        )
        query_order = lax.dynamic_slice_in_dim(order_rows, first_frame, frames_local, axis=1)
        time_visible = (order_rows[:, None, :] <= query_order[:, :, None])[:, None, :, :, None]
        time_q = queries_local.reshape(shape_heads)
        time_k = keys_all.reshape(shape_all)
        time_v = values_all.reshape(shape_all)
        total1, mixed_frames = time_forward(time_q, time_k, time_v, time_visible, scale)
        mixed1 = mixed_frames.reshape(row_count, joined_local)
        residual_stream2 = residual_stream1 + branch_out(mixed1, out_time)
        normalized_rows2, standardized_rows2, inverse_deviation2 = norm_forward_pass(
            residual_stream2, gain_broadcast[2], hidden_width
        )
        projected = jnp.dot(normalized_rows2, w_in, preferred_element_type=jnp.float32)
        activated, gelu_pull = jax.vjp(gelu_tanh, projected)
        hidden = activated.astype(jnp.bfloat16)
        resid3 = residual_stream2 + branch_out(hidden, w_out)
        outputs.append(
            resid3.astype(jnp.bfloat16).reshape(clips_local, frames_local, patches, cols_local)
        )
        grad3 = jnp.where(masked[:, None], upstream, 0.0)
        grad_hidden, grad_w_out = branch_back(grad3, hidden, w_out)
        grad_inner = gelu_pull(grad_hidden)[0].astype(jnp.bfloat16)
        grad_w_in = jnp.einsum(
            "rd,rk->dk", normalized_rows2, grad_inner, preferred_element_type=jnp.float32
        )
        normalized_gradient2 = sum_features(
            jnp.einsum("rk,dk->rd", grad_inner, w_in, preferred_element_type=jnp.float32)
        )
        backward_third, gain_gradient2 = norm_reverse_pass(
            normalized_gradient2,
            standardized_rows2,
            inverse_deviation2,
            gain_broadcast[2],
            hidden_width,
        )
        grad2 = grad3 + backward_third
        grad_mixed1, grad_out_time = branch_back(grad2, mixed1, out_time)
        grad_mixed_low = grad_mixed1.astype(jnp.bfloat16).reshape(shape_local)
        grad_queries, grad_keys, grad_values = time_backward(
            grad_mixed_low, time_q, time_k, time_v, time_visible, total1, scale
        )
        key_part, value_part = (
            lax.psum_scatter(
                grad_keys.reshape(clips_local, frames_all, patches, joined_local).astype(
                    jnp.bfloat16
                ),
                "tm",
                scatter_dimension=1,
                tiled=True,
            ).astype(jnp.float32),
            lax.psum_scatter(
                grad_values.reshape(clips_local, frames_all, patches, joined_local).astype(
                    jnp.bfloat16
                ),
                "tm",
                scatter_dimension=1,
                tiled=True,
            ).astype(jnp.float32),
        )
        grad_joined1 = jnp.stack(
            [
                grad_queries.reshape(row_count, joined_local),
                key_part.reshape(row_count, joined_local),
                value_part.reshape(row_count, joined_local),
            ]
        ).astype(jnp.bfloat16)
        grad_qkv_time, normalized_gradient1 = qkv_back(normalized_rows1, grad_joined1, qkv_time)
        backward_second, gain_gradient1 = norm_reverse_pass(
            normalized_gradient1,
            standardized_rows1,
            inverse_deviation1,
            gain_broadcast[1],
            hidden_width,
        )
        grad1 = grad2 + backward_second
        grad_mixed0, grad_out_space = branch_back(grad1, mixed0, out_space)
        grad_joined0 = space_backward(
            grad_mixed0.astype(jnp.bfloat16),
            joined0,
            total0,
            clips_local * frames_local,
            patches,
            heads_local,
            scale,
        )
        grad_qkv_space, normalized_gradient0 = qkv_back(normalized_rows0, grad_joined0, qkv_space)
        backward_first, gain_gradient0 = norm_reverse_pass(
            normalized_gradient0,
            standardized_rows0,
            inverse_deviation0,
            gain_broadcast[0],
            hidden_width,
        )
        grad0 = grad1 + backward_first
        input_grads.append(
            jnp.where(masked[:, None], 0.0, grad0).reshape(
                clips_local, frames_local, patches, cols_local
            )
        )
        grad_embed = jnp.sum(jnp.where(masked[:, None], grad0, 0.0), axis=0)
        gain_grads = jnp.stack([gain_gradient0, gain_gradient1, gain_gradient2])
        local_grads = (
            grad_qkv_space,
            grad_out_space,
            grad_qkv_time,
            grad_out_time,
            grad_w_in,
            grad_w_out,
        )
        small_grads = (gain_grads, grad_embed)
        reduced, reduced_small = reduce_grads(local_grads, small_grads)
        if weight_total is None:
            weight_total = reduced
            small_total = reduced_small
        else:
            weight_total = tuple((total + grad for total, grad in zip(weight_total, reduced)))
            small_total = tuple((total + grad for total, grad in zip(small_total, reduced_small)))
    return (
        jnp.concatenate(outputs, axis=0),
        jnp.concatenate(input_grads, axis=0),
        small_total[1],
        small_total[0],
        weight_total[0],
        weight_total[1],
        weight_total[2],
        weight_total[3],
        weight_total[4],
        weight_total[5],
    )


AXES = ("tm", "x", "c", "mp")
F32 = jnp.float32
BF16 = jnp.bfloat16
BLK = 256
MESH = pl.DeviceIdType.MESH


def device_pairs(move):
    pairs = []
    for y in range(2):
        for x in range(2):
            for c in range(2):
                for z in range(4):
                    there = move(y, x, c, z)
                    pairs.append(tuple(((q[0] * 2 + q[1]) * 2 + q[2]) * 4 + q[3] for q in ((y, x, c, z), there)))
    return pairs


def hop_y(v):
    return lax.ppermute(v, AXES, device_pairs(lambda y, x, c, z: (1 - y, x, c, z)))


def hop_x(v):
    return lax.ppermute(v, AXES, device_pairs(lambda y, x, c, z: (y, 1 - x, c, z)))


def hop_c(v):
    return lax.ppermute(v, AXES, device_pairs(lambda y, x, c, z: (y, x, 1 - c, z)))


def hop_z(v, shift):
    return lax.ppermute(v, AXES, device_pairs(lambda y, x, c, z: (y, x, c, (z + shift) % 4)))


def spread_pairs(r):
    def move(y, x, c, z):
        k = z ^ r
        return (y, x, k & 1, 2 * c + (k >> 1))

    return device_pairs(move)


def dot_nn(a, b):
    return lax.dot_general(a, b, (((1,), (0,)), ((), ())), preferred_element_type=F32)


def dot_nt(a, b):
    return lax.dot_general(a, b, (((1,), (1,)), ((), ())), preferred_element_type=F32)


def dot_tn(a, b):
    return lax.dot_general(a, b, (((0,), (0,)), ((), ())), preferred_element_type=F32)


def attend_pair(q, k, v, bias, scale):
    mixed, totals = [], []
    for i in range(2):
        mine = slice(i * HEAD_DIM, (i + 1) * HEAD_DIM)
        scores = dot_nt(k[:, mine], q[:, mine]) * scale
        if bias is not None:
            scores = scores + bias
        highest = jnp.max(scores, axis=0, keepdims=True)
        exponent = jnp.exp(scores - highest)
        total = jnp.sum(exponent, axis=0, keepdims=True)
        totals.append(highest + jnp.log(total))
        mixed.append(dot_tn(v[:, mine], exponent.astype(BF16)) * (1.0 / total))
    return (jnp.concatenate(mixed, axis=0).T, totals)


def attend_pair_back(q, k, v, g, totals, bias, scale):
    grads = ([], [], [])
    for i in range(2):
        mine = slice(i * HEAD_DIM, (i + 1) * HEAD_DIM)
        scores = dot_nt(k[:, mine], q[:, mine]) * scale
        if bias is not None:
            scores = scores + bias
        p = jnp.exp(scores - totals[i])
        dp = dot_nt(v[:, mine], g[:, mine])
        ds = (p * (dp - jnp.sum(p * dp, axis=0, keepdims=True))).astype(BF16)
        grads[0].append(dot_tn(k[:, mine], ds) * scale)
        grads[1].append(dot_nn(ds, q[:, mine]) * scale)
        grads[2].append(dot_nn(p.astype(BF16), g[:, mine]))
    return (
        jnp.concatenate(grads[0], axis=0).T,
        jnp.concatenate(grads[1], axis=1),
        jnp.concatenate(grads[2], axis=1),
    )


PAIR = 2 * HEAD_DIM


def enter_kernel(
    scale,
    tok, vec, qkv_hbm, out_hbm, time_hbm, time_out_hbm, feed_hbm, first_hbm, masked,
    wq_out, wo_out, wt, wf, wi, joined_out, turned_out, std_out,
    mixed, total_out, inverse, resid_out, next_out, inverse_next, low_out, vec_out,
    rows_in, vec_in, wq, wo, normed, joined, turned, std, base, part, part_out, part_in, resid, std_next, low_next,
    later, head_in, head_out,
    z_send, z_recv, y_send, y_recv, x_send, x_recv, p_send, p_recv, q_send, q_recv,
    t_send, t_recv, v_send, v_recv, u_send, u_recv, w_send, w_recv,
    f_send, f_recv, g_send, g_recv, n_send, n_recv, local, saved,
    i_send, i_recv, j_send, j_recv, k_send, k_recv, l_send, l_recv,
):
    y, x, c, z = (lax.axis_index(name) for name in AXES)
    half = wo.shape[0] // 4
    wide = 3 * half
    span = wt.shape[1] // 4
    size = wf.shape[1] // 4
    own = rows_in.shape[0]
    near_y, near_x, pair = (1 - y, x, c, z), (y, 1 - x, c, z), (y, x, 1 - c, z)
    right_z, left_z = (y, x, c, (z + 1) % 4), (y, x, c, (z + 3) % 4)

    def at(i, length):
        return pl.ds(pl.multiple_of(i * length, length), length)

    def remote(src, dst, send, recv, peer):
        return pltpu.make_async_remote_copy(
            src_ref=src, dst_ref=dst, send_sem=send, recv_sem=recv, device_id=peer, device_id_type=MESH
        )

    def start(all_copies):
        for copy in all_copies:
            copy.start()

    def landed(all_copies):
        for copy in all_copies:
            copy.wait_recv()

    def sent(all_copies):
        for copy in all_copies:
            copy.wait_send()

    core = at(c, half)
    keep = [
        pltpu.make_async_copy(
            qkv_hbm.at[j, :, core], wq.at[:, pl.ds(pl.multiple_of(z * wide + j * half, half), half)], local.at[j]
        )
        for j in range(3)
    ] + [pltpu.make_async_copy(out_hbm.at[core], wo.at[at(z, half)], local.at[3])]
    keep_later = [
        pltpu.make_async_copy(later, wt.at[:, at(z, span)], local.at[4]),
        pltpu.make_async_copy(feed_hbm.at[at(c, 4 * size)], wf.at[z], local.at[5]),
        pltpu.make_async_copy(first_hbm.at[:, at(c, 4 * size)], wi.at[z], local.at[8]),
    ]
    head = [
        pltpu.make_async_copy(time_hbm.at[:, :, at(y, PAIR)], head_in, local.at[9]),
        pltpu.make_async_copy(time_out_hbm.at[at(2 * y + c, HEAD_DIM)], head_out, local.at[10]),
    ]
    start(keep + keep_later[1:] + head)

    barrier = pltpu.get_barrier_semaphore()
    for dc in range(2):
        for dz in range(4):
            if dc or dz:
                peer = (y, x, (c + dc) % 2, (z + dz) % 4)
                pl.semaphore_signal(barrier, inc=1, device_id=peer, device_id_type=MESH)
    for peer in (near_y, near_x):
        pl.semaphore_signal(barrier, inc=1, device_id=peer, device_id_type=MESH)
    pl.semaphore_wait(barrier, 9)

    def spot(dy, dx):
        return 2 * ((y + dy) % 2) + (x + dx) % 2

    def piece(dy, dx, r, split=False):
        s = (z + r) % 4
        rows = at(spot(dy, dx), BLK)
        first = pl.multiple_of(s * wide, half)
        out = wo.at[at(s, half), at(spot(dy, dx), BLK)]
        if split:
            last = pl.multiple_of(s * wide + 2 * half, half)
            return (wq.at[rows, pl.ds(first, 2 * half)], wq.at[rows, pl.ds(last, half)], out)
        return (wq.at[rows, pl.ds(first, wide)], out)

    def time_piece(dx, r):
        return wt.at[at((x + dx) % 2, 2 * BLK), at((z + r) % 4, span)]

    def feed_piece(dy, r):
        return wf.at[(z + r) % 4, at(spot(dy, 0), size)]

    def copies(parts, send, recv, peer):
        return [remote(ref, ref, send.at[i], recv.at[i], peer) for i, ref in enumerate(parts)]

    def leg(right, step):
        if right:
            return (0 if step == 0 else 4 - step), right_z, 3 - step
        return step, left_z, step + 1

    def z_copies(right, step):
        r, peer, lands = leg(right, step)
        return copies(piece(0, 0, r), z_send.at[int(right), step], z_recv.at[lands], peer)

    def time_z(right, step):
        r, peer, lands = leg(right, step)
        source = later.at[at(x, 2 * BLK)] if step == 0 else time_piece(0, r)
        return [remote(source, time_piece(0, r), u_send.at[int(right), step], u_recv.at[lands], peer)]

    def feed_z(right, step):
        r, peer, lands = leg(right, step)
        source = feed_hbm.at[at(4 * c + spot(0, 0), size)] if step == 0 else feed_piece(0, r)
        return [remote(source, feed_piece(0, r), f_send.at[int(right), step], f_recv.at[lands], peer)]

    def first_piece(dy, dx, r):
        return wi.at[(z + r) % 4, at(spot(dy, dx), BLK)]

    def first_z(right, step):
        r, peer, lands = leg(right, step)
        source = first_hbm.at[at(spot(0, 0), BLK), at(c, 4 * size)] if step == 0 else first_piece(0, 0, r)
        return [remote(source, first_piece(0, 0, r), i_send.at[int(right), step], i_recv.at[lands], peer)]

    def first_y(r, dy=0):
        return [remote(first_piece(dy, 0, r), first_piece(dy, 0, r), j_send.at[r], j_recv.at[r], near_y)]

    def first_x(r, dx=0):
        return [remote(first_piece(0, dx, r), first_piece(0, dx, r), k_send.at[r], k_recv.at[r], near_x)]

    def y_copies(r, dy=0):
        return copies(piece(dy, 0, r), y_send.at[r], y_recv.at[r], near_y)

    def x_copies(r, dx=0):
        return copies(piece(0, dx, r), x_send.at[r], x_recv.at[r], near_x)

    def corner_x(r, dx=0):
        return copies(piece(1, dx, r, split=True)[:1], p_send.at[r], p_recv.at[r], near_x)

    def corner_y(r, dy=0):
        return copies(piece(dy, 1, r, split=True)[1:], q_send.at[r], q_recv.at[r], near_y)

    def time_x(r, dx=0):
        return [remote(time_piece(dx, r), time_piece(dx, r), w_send.at[r], w_recv.at[r], near_x)]

    def feed_y(r, dy=0):
        return [remote(feed_piece(dy, r), feed_piece(dy, r), g_send.at[r], g_recv.at[r], near_y)]

    def token_copies(k):
        peer = (y, x, k % 2, 2 * c + k // 2)
        return [
            remote(tok.at[k], rows_in.at[:, at(z, BLK)], t_send.at[k], t_recv.at[z], peer),
            remote(vec, vec_in.at[:, at(z, BLK)], v_send.at[k], v_recv.at[z], peer),
        ]

    def token_local(k):
        return [
            pltpu.make_async_copy(tok.at[k], rows_in.at[:, at(z, BLK)], local.at[6]),
            pltpu.make_async_copy(vec, vec_in.at[:, at(z, BLK)], local.at[7]),
        ]

    def stays(k):
        return jnp.logical_and(2 * c + k // 2 == z, c == k % 2)

    def start_tokens(ks):
        for k in ks:
            pl.when(stays(k))(lambda k=k: start(token_local(k)))
            pl.when(jnp.logical_not(stays(k)))(lambda k=k: start(token_copies(k)))

    def each_side(j, act):
        pl.when(z >= j + 1)(lambda: act(3 - j, True))
        pl.when(z <= 2 - j)(lambda: act(j + 1, False))

    def begin(make):
        pl.when(z < 3)(lambda: start(make(True, 0)))
        pl.when(z > 0)(lambda: start(make(False, 0)))

    def onward(j, make, right):
        if j < 2:
            pl.when(z < 3 if right else z > 0)(lambda: start(make(right, j + 1)))

    def forward(j):
        def act(r, right):
            landed(copies(piece(0, 0, r), z_send.at[0, 0], z_recv.at[r], near_y))
            onward(j, z_copies, right)
            start(y_copies(r))
            start(x_copies(r))

        each_side(j, act)

    def corners(j):
        def act(r, right):
            landed(y_copies(r, 1))
            start(corner_x(r))
            landed(x_copies(r, 1))
            start(corner_y(r))

        each_side(j, act)

    def time_forward_step(j):
        def act(r, right):
            landed([remote(time_piece(0, r), time_piece(0, r), u_send.at[0, 0], u_recv.at[r], near_x)])
            onward(j, time_z, right)
            start(time_x(r))

        each_side(j, act)

    def feed_forward_step(j):
        def act(r, right):
            landed([remote(feed_piece(0, r), feed_piece(0, r), f_send.at[0, 0], f_recv.at[r], near_y)])
            onward(j, feed_z, right)
            start(feed_y(r))

        each_side(j, act)

    def first_corner_copy(r, dx=0):
        return [remote(first_piece(1, dx, r), first_piece(1, dx, r), l_send.at[r], l_recv.at[r], near_x)]

    def first_corner(j):
        def act(r, right):
            landed(first_y(r, 1))
            start(first_corner_copy(r))

        each_side(j, act)

    def first_forward_step(j):
        def act(r, right):
            landed([remote(first_piece(0, 0, r), first_piece(0, 0, r), i_send.at[0, 0], i_recv.at[r], near_y)])
            onward(j, first_z, right)
            start(first_y(r))
            start(first_x(r))

        each_side(j, act)

    for copy in keep:
        copy.wait()
    begin(z_copies)

    def gather_head(i, carry):
        rows = at(i, BLK)
        parts = [head_in[j, rows].astype(F32) for j in range(3)]
        parts = [jnp.where(c == 0, v[:, :HEAD_DIM], v[:, HEAD_DIM:]) for v in parts]
        parts.append(head_out[:, rows].astype(F32).T)
        later[rows] = jnp.concatenate(parts, axis=1).astype(BF16)
        return carry

    for copy in head:
        copy.wait()
    lax.fori_loop(0, later.shape[0] // BLK, gather_head, 0)
    keep_later[0].start()
    forward(0)
    start_tokens((0, 1))
    forward(1)
    start_tokens((2, 3))
    begin(first_z)
    begin(time_z)
    begin(feed_z)
    corners(0)
    forward(2)
    corners(1)
    for k in range(4):
        def finish_local(k=k):
            for copy in token_local(k):
                copy.wait()

        pl.when(stays(k))(finish_local)
    for s in range(4):
        def arrived(s=s):
            landed([
                remote(tok.at[0], rows_in.at[:, at(s, BLK)], t_send.at[0], t_recv.at[s], near_y),
                remote(vec, vec_in.at[:, at(s, BLK)], v_send.at[0], v_recv.at[s], near_y),
            ])

        pl.when(jnp.logical_not(jnp.logical_and(z == s, z // 2 == c)))(arrived)

    step = own // 2
    slab = 128
    vec_out[...] = vec_in[...].astype(F32)

    def first_norm(i, carry):
        rows = at(i, step)
        value = jnp.where(masked[rows] > 0.0, vec_out[0:1], rows_in[rows].astype(F32))
        base[rows] = value
        standard, inv = norm_rows(value)
        std[rows] = standard
        inverse[rows] = inv
        normed[rows] = (standard * vec_out[1:2]).astype(BF16)
        return carry

    lax.fori_loop(0, 2, first_norm, 0)
    give_normed = remote(normed.at[pl.ds(0, own)], normed.at[pl.ds(own, own)], n_send.at[0], n_recv.at[0], pair)
    give_normed.start()
    corners(2)

    def turn(i, carry):
        turned[:, at(i, slab)] = normed[at(i, slab)].T
        return carry

    lax.fori_loop(0, own // slab, turn, 0)
    for r in (1, 2, 3):
        landed(corner_x(r, 1))
        landed(corner_y(r, 1))
    saves = [
        pltpu.make_async_copy(wq, wq_out, saved.at[0]),
        pltpu.make_async_copy(wo, wo_out, saved.at[1]),
        pltpu.make_async_copy(std, std_out, saved.at[2]),
    ]
    start(saves)
    first_forward_step(0)

    def attend(i, carry):
        rows = at(i, slab)
        for h in range(wo.shape[0] // PAIR):
            q, k, v = (joined[rows, (3 * h + j) * PAIR : (3 * h + j + 1) * PAIR] for j in range(3))
            out, totals = attend_pair(q, k, v, None, scale)
            mixed[rows, h * PAIR : (h + 1) * PAIR] = out.astype(BF16)
            for j in range(2):
                total_out[i, 2 * h + j : 2 * h + j + 1, :] = totals[j]
        return carry

    def project(t):
        rows = pl.ds(t * own, own)
        joined[rows] = dot_nn(normed[rows], wq[...]).astype(BF16)

    frames = own // slab
    project(0)
    time_forward_step(0)
    lax.fori_loop(0, frames, attend, 0)
    part[...] = dot_nn(mixed[pl.ds(0, own)], wo[...])
    feed_forward_step(0)
    first_forward_step(1)
    first_corner(0)
    give_normed.wait_recv()
    project(1)
    saves.append(pltpu.make_async_copy(joined, joined_out, saved.at[3]))
    saves[3].start()
    lax.fori_loop(frames, 2 * frames, attend, 0)
    part_out[...] = dot_nn(mixed[pl.ds(own, own)], wo[...]).astype(BF16)
    give_part = remote(part_out, part_in, n_send.at[1], n_recv.at[1], pair)
    give_part.start()
    time_forward_step(1)
    feed_forward_step(1)
    first_corner(1)
    lax.fori_loop(own // slab, 2 * own // slab, turn, 0)
    saves.append(pltpu.make_async_copy(turned, turned_out, saved.at[4]))
    saves[4].start()
    give_part.wait_recv()
    first_forward_step(2)

    def second_norm(i, carry):
        rows = at(i, step)
        value = base[rows] + part[rows] + part_in[rows].astype(F32)
        resid[rows] = value
        standard, inv = norm_rows(value)
        std_next[rows] = standard
        inverse_next[rows] = inv
        low_next[rows] = (standard * vec_out[2:3]).astype(BF16)
        return carry

    lax.fori_loop(0, 2, second_norm, 0)
    for i, (src, dst) in enumerate(((resid, resid_out), (std_next, next_out), (low_next, low_out))):
        saves.append(pltpu.make_async_copy(src, dst, saved.at[5 + i]))
        saves[-1].start()
    time_forward_step(2)
    feed_forward_step(2)

    def first_ends(j):
        def act(r, right):
            if j == 2:
                landed(first_y(r, 1))
            else:
                landed(first_corner_copy(r, 1))
                sent(first_corner_copy(r))

        each_side(j, act)

    for j in range(3):
        first_ends(j)
    for copy in keep_later + saves:
        copy.wait()
    give_normed.wait_send()
    give_part.wait_send()
    for r in (1, 2, 3):
        landed(time_x(r, 1))
        landed(feed_y(r, 1))
        landed(first_x(r, 1))
        for group in (y_copies(r), x_copies(r), corner_x(r), corner_y(r), time_x(r), feed_y(r), first_y(r), first_x(r)):
            sent(group)
    for step_z in range(3):
        for make in (z_copies, time_z, first_z, feed_z):
            pl.when(jnp.logical_and(z >= step_z, z < 3))(lambda step_z=step_z, make=make: sent(make(True, step_z)))
            pl.when(jnp.logical_and(z + step_z <= 3, z > 0))(lambda step_z=step_z, make=make: sent(make(False, step_z)))
    for k in range(4):
        pl.when(jnp.logical_not(stays(k)))(lambda k=k: sent(token_copies(k)))


def enter(tok, vec, qkv, out, time_qkv, time_out, feed_weight, first_weight, masked, scale):
    own, width, half = tok.shape[1], 4 * tok.shape[2], out.shape[0] // 2
    size = feed_weight.shape[0] // 2
    dma = pltpu.SemaphoreType.DMA
    anywhere = pl.BlockSpec(memory_space=pl.ANY)
    whole = pl.BlockSpec(memory_space=pltpu.VMEM)
    heads = 4 * half // HEAD_DIM

    def low(*shape):
        return pltpu.VMEM(shape, BF16)

    def high(*shape):
        return pltpu.VMEM(shape, F32)

    shapes = [
        ((width, 12 * half), BF16), ((4 * half, width), BF16), ((width, 16 * HEAD_DIM), BF16),
        ((4, size, width), BF16), ((4, width, size), BF16), ((2 * own, 12 * half), BF16), ((width, 2 * own), BF16), ((own, width), F32),
        ((2 * own, 4 * half), BF16), ((2 * own // 128, heads, 128), F32), ((own, 1), F32), ((own, width), F32),
        ((own, width), F32), ((own, 1), F32), ((own, width), BF16), ((vec.shape[0], width), F32),
    ]
    return pl.pallas_call(
        functools.partial(enter_kernel, scale),
        in_specs=[anywhere] * 8 + [whole],
        out_specs=[anywhere] * 8 + [whole] * 3 + [anywhere] * 2 + [whole, anywhere, whole],
        out_shape=[jax.ShapeDtypeStruct(shape, kind) for shape, kind in shapes],
        scratch_shapes=[
            low(own, width), low(vec.shape[0], width), low(width, 12 * half), low(4 * half, width),
            low(2 * own, width), low(2 * own, 12 * half), low(width, 2 * own), high(own, width), high(own, width),
            high(own, width), low(own, width), low(own, width), high(own, width), high(own, width), low(own, width),
            low(width, 4 * HEAD_DIM), low(3, width, PAIR), low(HEAD_DIM, width),
            dma((2, 3, 2)), dma((4, 2)), dma((4, 2)), dma((4, 2)), dma((4, 2)), dma((4, 2)),
            dma((4, 1)), dma((4, 1)), dma((4, 2)), dma((4, 2)),
            dma((4,)), dma((4,)), dma((4,)), dma((4,)), dma((2, 3)), dma((4,)), dma((4,)), dma((4,)),
            dma((2, 3)), dma((4,)), dma((4,)), dma((4,)), dma((2,)), dma((2,)), dma((11,)), dma((8,)),
            dma((2, 3)), dma((4,)), dma((4,)), dma((4,)), dma((4,)), dma((4,)), dma((4,)), dma((4,)),
        ],
        compiler_params=pltpu.CompilerParams(
            collective_id=0, has_side_effects=True, vmem_limit_bytes=56 * 1024 * 1024
        ),
        cost_estimate=pl.CostEstimate(flops=10**10, transcendentals=10**6, bytes_accessed=10**8),
        name="enter",
    )(tok, vec, qkv, out, time_qkv, time_out, feed_weight, first_weight, masked)


GROUP = 8
CHUNK = 16


def time_kernel(back, scale, heads, *refs):
    if back:
        (own_ref, rider_ref, joined_hbm, total_ref, wide_ref, turned_ref, mixed_hbm, wt_hbm, bias_ref) = refs[:9]
        (delta_ref, grad_ref, reduced_ref, rider_out) = refs[9:13]
        (half_in, half_own, line_out, line_in, half_send, half_recv, half_local, line_send, line_recv) = refs[-17:-8]
        (out_ref, turned, grad_qkv, grad_out, wt_ref, joined_ref, mixed_ref, load_sem) = refs[-8:]
        refs = refs[13:-17]
    else:
        (own_ref, rider_ref, far_ref, in_ref, wt_hbm, bias_ref) = refs[:6]
        (turned_ref, out_ref, mixed_ref, total_ref, delta_ref, rider_out, spread_out, in_out) = refs[6:14]
        (turned, wt_ref, load_sem) = refs[-3:]
        refs = refs[14:-3]
    (
        wq_ref, wo_ref, held, wide, narrow, kept, core_out, core_in, near_out, near_in,
        gy_send, gy_recv, gc_send, gc_recv, gd_send, gd_recv, sc_send, sc_recv, sy_send, sy_recv,
        r_send, r_recv, r_local, out_sem, wx_send, wx_recv,
    ) = refs
    y, x, c, z = (lax.axis_index(name) for name in AXES)
    near, pair, near_x = (1 - y, x, c, z), (y, x, 1 - c, z), (y, 1 - x, c, z)
    frames = held.shape[0] // 4
    chunks = held.shape[1] // CHUNK
    width = heads * HEAD_DIM
    groups = CHUNK // GROUP

    loads = [(wt_hbm, wt_ref), (own_ref, held.at[pl.ds(0, frames)])]
    if back:
        loads += [(joined_hbm, joined_ref), (mixed_hbm, mixed_ref)]
    loads = [pltpu.make_async_copy(src, dst, load_sem.at[i]) for i, (src, dst) in enumerate(loads)]
    for copy in loads:
        copy.start()
    barrier = pltpu.get_barrier_semaphore()
    for dc in range(2):
        for dz in range(4):
            if dc or dz:
                pl.semaphore_signal(barrier, inc=1, device_id=(y, x, (c + dc) % 2, (z + dz) % 4), device_id_type=MESH)
    pl.semaphore_signal(barrier, inc=1, device_id=near, device_id_type=MESH)
    pl.semaphore_signal(barrier, inc=1, device_id=near_x, device_id_type=MESH)
    pl.semaphore_wait(barrier, 9)

    def remote(src, dst, send, recv, peer):
        return pltpu.make_async_remote_copy(
            src_ref=src, dst_ref=dst, send_sem=send, recv_sem=recv, device_id=peer, device_id_type=MESH
        )

    def patches(k):
        return pl.ds(pl.multiple_of(k * CHUNK, CHUNK), CHUNK)

    def block(b, k):
        return held.at[pl.ds(b * frames, frames), patches(k)]

    def gather_y(k):
        return remote(own_ref.at[:, patches(k)], block(1, k), gy_send.at[k], gy_recv.at[k], near)

    def gather_c(k):
        return remote(own_ref.at[:, patches(k)], block(2, k), gc_send.at[k], gc_recv.at[k], pair)

    def gather_d(k):
        return remote(block(1, k), block(3, k), gd_send.at[k], gd_recv.at[k], pair)

    def scatter_c(k):
        return remote(core_out.at[k], core_in.at[k], sc_send.at[k], sc_recv.at[k], pair)

    def scatter_y(k):
        return remote(near_out.at[k], near_in.at[k], sy_send.at[k], sy_recv.at[k], near)

    def save(k):
        there = (turned_ref.at[k], turned.at[k]) if back else (turned.at[k], turned_ref.at[k])
        return pltpu.make_async_copy(*there, out_sem.at[k])

    def columns(s):
        return pl.ds(pl.multiple_of(s * BLK, BLK), BLK)

    def stays(k):
        if back:
            return jnp.logical_and(z == k, z // 2 == c)
        return jnp.logical_and(2 * c + k // 2 == z, c == k % 2)

    def ride(k):
        if back:
            src, dst = rider_ref.at[:, columns(k)], rider_out.at[2 * (z % 2) + c]
            peer, slot = (y, x, z // 2, k), 2 * (z % 2) + c
        else:
            src, dst = rider_ref.at[k], rider_out.at[:, columns(z)]
            peer, slot = (y, x, k % 2, 2 * c + k // 2), z
        return src, dst, peer, slot

    def ride_remote(k):
        src, dst, peer, slot = ride(k)
        return remote(src, dst, r_send.at[k], r_recv.at[slot], peer)

    def ride_local(k):
        src, dst, _, _ = ride(k)
        return pltpu.make_async_copy(src, dst, r_local.at[0])

    def ride_landed(k):
        if back:
            src, dst = rider_ref.at[:, columns(k)], rider_out.at[k]
        else:
            src, dst = rider_ref.at[k], rider_out.at[:, columns(k)]
        return remote(src, dst, r_send.at[k], r_recv.at[k], near)

    def from_self(k):
        if back:
            return jnp.logical_and(2 * c + k // 2 == z, c == k % 2)
        return jnp.logical_and(z == k, z // 2 == c)

    def spread_x(i, dx=0):
        r, yb = i // 2 + 1, i % 2
        size = far_ref.shape[1] // 4
        at = pl.multiple_of(size * (2 * yb + (x + dx) % 2), size)
        src = far_ref.at[(z + r) % 4, pl.ds(at, size)]
        return remote(src, spread_out.at[(z + r) % 4, pl.ds(at, size)], wx_send.at[i], wx_recv.at[i], near_x)

    gather_y(0).start()
    for k in range(chunks):
        if k > 0:
            gather_y(k).start()
        gather_c(k).start()
    def spread_in(dx=0):
        at = pl.multiple_of(BLK * (2 * (1 - y) + (x + dx) % 2), BLK)
        there = in_out.at[3 - z, pl.ds(at, BLK)]
        return remote(in_ref.at[3 - z, pl.ds(at, BLK)], there, wx_send.at[6], wx_recv.at[6], near_x)

    at_end = jnp.logical_or(z == 0, z == 3)

    def half_away(s):
        return remote(wide_ref.at[1 - x, s], half_in.at[s], half_send.at[s], half_recv.at[s], near_x)

    def half_here(s):
        return pltpu.make_async_copy(wide_ref.at[x, s], half_own.at[s], half_local.at[s])

    def line_away(r):
        return remote(line_out.at[r], line_in.at[r], line_send.at[r], line_recv.at[r], (y, x, c, (z + r) % 4))

    def halve():
        for s in range(4):
            half_away(s).wait_recv()
            half_here(s).wait()
        for r in range(4):
            s = (z + r) % 4
            whole = half_own[s].astype(F32) + half_in[s].astype(F32)
            if r == 0:
                reduced_ref[...] = whole
            else:
                line_out[r] = whole.astype(BF16)
                line_away(r).start()

    if back:
        for s in range(4):
            half_away(s).start()
            half_here(s).start()
    else:
        pl.when(at_end)(lambda: spread_in().start())
        for i in range(6):
            spread_x(i).start()
    for k in range(4):
        pl.when(stays(k))(lambda k=k: ride_local(k).start())
        pl.when(jnp.logical_not(stays(k)))(lambda k=k: ride_remote(k).start())
    if back:
        for k in range(chunks):
            save(k).start()

    def assemble(i, carry):
        rows = pl.ds(pl.multiple_of(i * BLK, BLK), BLK)
        for s in range(0, heads, 2):
            for part in range(4):
                both = [
                    wt_ref[rows, (s + j) * 4 * HEAD_DIM + part * HEAD_DIM : (s + j) * 4 * HEAD_DIM + (part + 1) * HEAD_DIM]
                    for j in range(2)
                ]
                both = jnp.concatenate(both, axis=1)
                if part < 3:
                    wq_ref[rows, part * width + s * HEAD_DIM : part * width + s * HEAD_DIM + PAIR] = both
                else:
                    wo_ref[rows, s * HEAD_DIM : s * HEAD_DIM + PAIR] = both
        return carry

    loads[0].wait()
    lax.fori_loop(0, wt_ref.shape[0] // BLK, assemble, 0)
    for copy in loads[1:]:
        copy.wait()

    def finish(k):
        scatter_c(k).wait_recv()
        both = kept[:, patches(k)] + core_in[k].astype(F32)
        near_out[k] = both[frames:].astype(BF16)
        delta_ref[:, patches(k)] = both[:frames]
        scatter_y(k).start()

    def pass_on(k):
        gather_y(k).wait_recv()
        gather_d(k).start()

    def one_group(i, rows):
        at = pl.ds(pl.multiple_of(i * GROUP, GROUP), GROUP)
        count = 4 * frames * GROUP
        bias = bias_ref[...]
        for lo in range(0, width, PAIR):
            q, k, v = (
                wide[:, at, part * width + lo : part * width + lo + PAIR].reshape(count, PAIR).astype(BF16)
                for part in range(3)
            )
            h = lo // HEAD_DIM
            if back:
                g = narrow[:, at, lo : lo + PAIR].reshape(count, PAIR).astype(BF16)
                totals = [total_ref[rows * groups + i, h + j : h + j + 1, :] for j in range(2)]
                grads = attend_pair_back(q, k, v, g, totals, bias, scale)
                for part in range(3):
                    wide[:, at, part * width + lo : part * width + lo + PAIR] = grads[part].reshape(
                        4 * frames, GROUP, PAIR
                    )
            else:
                mixed, totals = attend_pair(q, k, v, bias, scale)
                narrow[:, at, lo : lo + PAIR] = mixed.reshape(4 * frames, GROUP, PAIR)
                for j in range(2):
                    total_ref[rows * groups + i, h + j : h + j + 1, :] = totals[j]

    def one_chunk(k, carry):
        pl.when(k + 1 < chunks)(lambda: pass_on(k + 1))
        gather_c(k).wait_recv()
        gather_d(k).wait_recv()
        count = 4 * frames * CHUNK
        lhs = held[:, patches(k)].reshape(count, held.shape[2])
        if back:
            wide[...] = joined_ref[:, patches(k)].astype(F32)
            narrow[...] = dot_nn(lhs, wo_ref[...]).astype(BF16).astype(F32).reshape(narrow.shape)
        else:
            joined = dot_nn(lhs, wq_ref[...]).astype(BF16)
            out_ref[:, patches(k)] = joined.reshape(wide.shape)
            wide[...] = joined.astype(F32).reshape(wide.shape)
        lax.fori_loop(0, groups, lambda i, carry: (one_group(i, k), carry)[1], 0)
        if back:
            grads = wide[...].astype(BF16)
            out_ref[:, patches(k)] = grads
            partial = dot_nt(grads.reshape(count, 3 * width), wq_ref[...])
        else:
            mixed = narrow[...].astype(BF16)
            mixed_ref[:, patches(k)] = mixed
            partial = dot_nt(mixed.reshape(count, width), wo_ref[...])
        partial = partial.reshape(4 * frames, CHUNK, held.shape[2])
        kept[:, patches(k)] = partial[: 2 * frames]
        core_out[k] = partial[2 * frames :].astype(BF16)
        scatter_c(k).start()
        pl.when(k > 0)(lambda: finish(k - 1))
        if not back:
            for b in range(4):
                slab = held[b * frames : (b + 1) * frames, patches(k)].reshape(frames * CHUNK, held.shape[2])
                turned[k, :, b * frames * CHUNK : (b + 1) * frames * CHUNK] = slab.T
            save(k).start()
        if back:
            pl.when(k == chunks // 2 - 1)(halve)
        return carry

    pass_on(0)
    lax.fori_loop(0, chunks, one_chunk, 0)
    finish(chunks - 1)

    def weigh(k, carry):
        count = 4 * frames * CHUNK
        save(k).wait()
        grad_qkv[...] = grad_qkv[...] + dot_nn(turned[k], out_ref[:, patches(k)].reshape(count, 3 * width))
        grad_out[...] = grad_out[...] + dot_tn(
            mixed_ref[:, patches(k)].reshape(count, width), held[:, patches(k)].reshape(count, held.shape[2])
        )
        return carry

    def arrange(i, carry):
        rows = pl.ds(pl.multiple_of(i * BLK, BLK), BLK)
        last = grad_out[:, rows].T
        for s in range(heads):
            mine = slice(s * HEAD_DIM, (s + 1) * HEAD_DIM)
            parts = [grad_qkv[rows, j * width : (j + 1) * width][:, mine] for j in range(3)] + [last[:, mine]]
            grad_ref[rows, 2 * s * PAIR : (2 * s + 1) * PAIR] = jnp.concatenate(parts[:2], axis=1).astype(BF16)
            grad_ref[rows, (2 * s + 1) * PAIR : (2 * s + 2) * PAIR] = jnp.concatenate(parts[2:], axis=1).astype(BF16)
        return carry

    if back:
        grad_qkv[...] = jnp.zeros_like(grad_qkv)
        grad_out[...] = jnp.zeros_like(grad_out)
        lax.fori_loop(0, chunks, weigh, 0)
        lax.fori_loop(0, grad_ref.shape[0] // BLK, arrange, 0)
    for k in range(chunks):
        scatter_y(k).wait_recv()
        delta_ref[:, patches(k)] = delta_ref[:, patches(k)] + near_in[k].astype(F32)
    if back:
        for r in (1, 2, 3):
            line_away(r).wait_recv()
            reduced_ref[...] = reduced_ref[...] + line_in[r].astype(F32)
        for r in (1, 2, 3):
            line_away(r).wait_send()
        for s in range(4):
            half_away(s).wait_send()
    for k in range(chunks):
        for copy in (gather_y(k), gather_c(k), gather_d(k), scatter_c(k), scatter_y(k)):
            copy.wait_send()
        if not back:
            save(k).wait()
    if not back:
        for i in range(6):
            spread_x(i, 1).wait_recv()
            spread_x(i).wait_send()

        def spread_in_end():
            spread_in(1).wait_recv()
            spread_in().wait_send()

        pl.when(at_end)(spread_in_end)
    for k in range(4):
        pl.when(stays(k))(lambda k=k: ride_local(k).wait())
        pl.when(jnp.logical_not(stays(k)))(lambda k=k: ride_remote(k).wait_send())
        pl.when(jnp.logical_not(from_self(k)))(lambda k=k: ride_landed(k).wait_recv())


def time_call(back, own, rider, saved, weights, bias, scale):
    frames, patches, features = own.shape
    width = weights.shape[1] // 4
    heads = width // HEAD_DIM
    chunks = patches // CHUNK
    rows = 4 * frames * GROUP
    dma = pltpu.SemaphoreType.DMA
    anywhere = pl.BlockSpec(memory_space=pl.ANY)
    whole = pl.BlockSpec(memory_space=pltpu.VMEM)
    turned = (chunks, features, 4 * frames * CHUNK)
    if back:
        out_shape = []
    else:
        out_shape = [
            jax.ShapeDtypeStruct(turned, BF16),
            jax.ShapeDtypeStruct((4 * frames, patches, 3 * width), BF16),
            jax.ShapeDtypeStruct((4 * frames, patches, width), BF16),
            jax.ShapeDtypeStruct((patches // GROUP, heads, rows), F32),
        ]
    rider_shape = (4, frames * patches, BLK) if back else (frames * patches, features)
    out_shape += [
        jax.ShapeDtypeStruct((frames, patches, features), F32),
        jax.ShapeDtypeStruct(rider_shape, BF16),
    ]
    held = 2
    half = saved[2].shape[1:] if back else None
    if back:
        out_shape.insert(-1, jax.ShapeDtypeStruct((features, features), BF16))
        out_shape.insert(-1, jax.ShapeDtypeStruct(half[1:], F32))
    else:
        out_shape += [jax.ShapeDtypeStruct(w.shape, BF16) for w in saved]
        held = 4
    return pl.pallas_call(
        functools.partial(time_kernel, back, scale, heads),
        in_specs=[anywhere] * 2
        + ([anywhere, whole, anywhere, anywhere, anywhere] if back else [anywhere] * 2)
        + [anywhere, whole],
        out_specs=([] if back else [anywhere]) + [whole] * (len(out_shape) - held + back) + [anywhere] * (held - 1),
        out_shape=out_shape,
        scratch_shapes=[
            pltpu.VMEM((features, 3 * width), BF16),
            pltpu.VMEM((features, width), BF16),
            pltpu.VMEM((4 * frames, patches, features), BF16),
            pltpu.VMEM((4 * frames, CHUNK, 3 * width), F32),
            pltpu.VMEM((4 * frames, CHUNK, width), F32),
            pltpu.VMEM((2 * frames, patches, features), F32),
            pltpu.VMEM((chunks, 2 * frames, CHUNK, features), BF16),
            pltpu.VMEM((chunks, 2 * frames, CHUNK, features), BF16),
            pltpu.VMEM((chunks, frames, CHUNK, features), BF16),
            pltpu.VMEM((chunks, frames, CHUNK, features), BF16),
        ]
        + [dma((chunks,))] * 10
        + [dma((4,)), dma((4,)), dma((1,)), dma((chunks,))]
        + [dma((7,))] * 2
        + ([pltpu.VMEM(half, BF16)] * 4 + [dma((4,))] * 5 if back else [])
        + ([pltpu.VMEM((4 * frames, patches, 3 * width), BF16)] if back else [])
        + [pltpu.VMEM(turned, BF16)]
        + ([pltpu.VMEM((features, 3 * width), F32), pltpu.VMEM((width, features), F32)] if back else [])
        + [pltpu.VMEM(weights.shape, BF16)]
        + ([pltpu.VMEM(saved[0].shape, BF16), pltpu.VMEM(saved[4].shape, BF16)] if back else [])
        + [dma((4,))],
        compiler_params=pltpu.CompilerParams(
            collective_id=2 if back else 1, has_side_effects=True, vmem_limit_bytes=60 * 1024 * 1024
        ),
        cost_estimate=pl.CostEstimate(flops=10**10, transcendentals=10**6, bytes_accessed=10**8),
        name="time_back" if back else "time_forward",
    )(own, rider, *saved, weights, bias)


def feed_kernel(
    resid_hbm, delta_hbm, upstream_hbm, masked, gain, w_in_hbm, w_in_far_hbm, w_out_hbm, w_far_hbm,
    half_in_hbm, half_out_hbm, grad_hbm, low_hbm, rows_hbm, gain_out,
    resid, delta, upstream, grad_out, low_out, rows_out, move_sem,
    w_in, w_out, standard, inverse, normed, grads, normed_t, grads_t, hidden, pulled, g_in, g_out, back, ahead,
    back_out, back_in, ahead_out, ahead_in, from_x, from_y, slopes,
    w_sem, g_sem, n_send, n_recv, b_send, b_recv, hx_send, hx_recv, hy_send, hy_recv,
):
    y, x, c, z = (lax.axis_index(name) for name in AXES)
    pair, near_y, near_x = (y, x, 1 - c, z), (1 - y, x, c, z), (y, 1 - x, c, z)
    own = resid.shape[0]
    moves = [
        pltpu.make_async_copy(src, dst, move_sem.at[i])
        for i, (src, dst) in enumerate((
            (resid_hbm, resid), (delta_hbm, delta), (upstream_hbm, upstream),
            (grad_out, grad_hbm), (low_out, low_hbm), (rows_out, rows_hbm),
        ))
    ]
    for copy in moves[:3]:
        copy.start()
    step = own // 2
    slab = 128

    def fetch(s, far, last=False):
        size = w_out.shape[1] // 4
        copies = []
        for i in range(4):
            rows = pl.ds(pl.multiple_of(BLK * (2 * ((y + i // 2) % 2) + (x + i % 2) % 2), BLK), BLK)
            source = w_in_far_hbm if last and i == 3 else w_in_hbm
            copies.append(pltpu.make_async_copy(source.at[s, rows], w_in.at[s, rows], w_sem.at[5 + i, s]))
        for i in range(4):
            rows = pl.ds(pl.multiple_of(size * (2 * (i // 2) + (x + i % 2) % 2), size), size)
            source = w_far_hbm if far and i % 2 else w_out_hbm
            copies.append(pltpu.make_async_copy(source.at[s, rows], w_out.at[s, rows], w_sem.at[i, s]))
        return copies

    def fetch_now(s, far, last):
        for copy in fetch(s, far, last):
            copy.start()

    for s in range(4):
        pl.when(z == s)(lambda s=s: fetch_now(s, False, False))
        if s in (0, 3):
            pl.when(z == 3 - s)(lambda s=s: fetch_now(s, True, True))
            pl.when(jnp.logical_and(z != s, z != 3 - s))(lambda s=s: fetch_now(s, True, False))
        else:
            pl.when(z != s)(lambda s=s: fetch_now(s, True, False))
    barrier = pltpu.get_barrier_semaphore()
    for peer in (pair, near_y, near_x):
        pl.semaphore_signal(barrier, inc=1, device_id=peer, device_id_type=MESH)

    def remote(src, dst, send, recv, peer=pair):
        return pltpu.make_async_remote_copy(
            src_ref=src, dst_ref=dst, send_sem=send, recv_sem=recv, device_id=peer, device_id_type=MESH
        )

    def block(yb, xb):
        return pl.ds(pl.multiple_of(BLK * (2 * yb + xb), BLK), BLK)

    def away_x(s, i):
        return remote(g_out.at[s, block(i, 1 - x)], from_x.at[i, s], hx_send.at[i, s], hx_recv.at[i, s], near_x)

    def away_y(s, i):
        return remote(g_in.at[s, block(1 - y, i)], from_y.at[i, s], hy_send.at[i, s], hy_recv.at[i, s], near_y)

    def keep(s, i):
        return (
            pltpu.make_async_copy(g_out.at[s, block(i, x)], half_out_hbm.at[i, s], g_sem.at[0, i, s]),
            pltpu.make_async_copy(g_in.at[s, block(y, i)], half_in_hbm.at[i, s], g_sem.at[1, i, s]),
        )

    def combine(s):
        for i in range(2):
            away_x(s, i).wait_recv()
            g_out[s, block(i, x)] = (g_out[s, block(i, x)].astype(F32) + from_x[i, s].astype(F32)).astype(BF16)
            away_y(s, i).wait_recv()
            g_in[s, block(y, i)] = (g_in[s, block(y, i)].astype(F32) + from_y[i, s].astype(F32)).astype(BF16)
            for copy in keep(s, i):
                copy.start()

    def at(i, size):
        return pl.ds(pl.multiple_of(i * size, size), size)

    def prepare(i, carry):
        rows = at(i, step)
        grads[rows] = jnp.where(masked[rows] > 0.0, upstream[rows].astype(F32), 0.0).astype(BF16)
        std, inv = norm_rows(resid[rows] + delta[rows])
        standard[rows] = std
        inverse[rows] = inv
        normed[rows] = (std * gain[3:4]).astype(BF16)
        return carry

    for copy in moves[:3]:
        copy.wait()
    lax.fori_loop(0, 2, prepare, 0)
    pl.semaphore_wait(barrier, 3)
    mine, theirs = pl.ds(0, own), pl.ds(own, own)
    give_grads = remote(grads.at[mine], grads.at[theirs], n_send.at[0], n_recv.at[0])
    give_normed = remote(normed.at[mine], normed.at[theirs], n_send.at[1], n_recv.at[1])
    give_normed.start()
    give_grads.start()

    def turn(i, carry):
        rows = at(i, slab)
        normed_t[:, rows] = normed[rows].T
        grads_t[:, rows] = grads[rows].T
        return carry

    lax.fori_loop(0, own // slab, turn, 0)
    rate = math.sqrt(2.0 / math.pi)

    def bend_step(s, rows):
        inner = dot_nn(normed[rows], w_in[s])
        square = inner * inner
        bend = jnp.tanh(rate * inner * (1.0 + 0.044715 * square))
        hidden[rows] = (0.5 * inner * (1.0 + bend)).astype(BF16)
        slopes[rows] = 0.5 * (1.0 + bend) + 0.5 * inner * (1.0 - bend * bend) * (rate * (1.0 + 3.0 * 0.044715 * square))

    def pull_step(s, rows):
        pulled[rows] = (dot_nt(grads[rows], w_out[s]) * slopes[rows]).astype(BF16)

    def add_step(s, rows):
        ahead[rows] = ahead[rows] + dot_nn(hidden[rows], w_out[s])
        back[rows] = back[rows] + dot_nt(pulled[rows], w_in[s])

    def clear():
        back[...] = jnp.zeros_like(back)
        ahead[...] = jnp.zeros_like(ahead)

    def meet():
        give_normed.wait_recv()
        give_grads.wait_recv()
        lax.fori_loop(own // slab, 2 * own // slab, turn, 0)

    def one_piece(s, carry):
        for copy in fetch(s, False):
            copy.wait()

        def first_half(t, carry):
            pl.when(jnp.logical_and(s == 0, t == 1))(meet)
            bend_step(s, at(t, own))
            return carry

        lax.fori_loop(0, 2, first_half, 0)
        g_out[s] = dot_nn(grads_t[...], hidden[...]).astype(BF16)
        for i in range(2):
            away_x(s, i).start()
        lax.fori_loop(0, 2, lambda t, carry: (pull_step(s, at(t, own)), carry)[1], 0)
        g_in[s] = dot_nn(normed_t[...], pulled[...]).astype(BF16)
        for i in range(2):
            away_y(s, i).start()
        pl.when(s == 0)(clear)
        lax.fori_loop(0, 2, lambda t, carry: (add_step(s, at(t, own)), carry)[1], 0)
        return carry

    lax.fori_loop(0, 4, one_piece, 0)
    back_out[...] = back[theirs].astype(BF16)
    give_back = remote(back_out, back_in, b_send.at[0], b_recv.at[0])
    give_back.start()
    ahead_out[...] = ahead[theirs].astype(BF16)
    give_ahead = remote(ahead_out, ahead_in, b_send.at[1], b_recv.at[1])
    give_ahead.start()
    give_back.wait_recv()

    def finish(i, total):
        rows = at(i, step)
        grad = back[rows] + back_in[rows].astype(F32)
        std = standard[rows]
        inner = grad * gain[3:4]
        mean = jnp.mean(inner, axis=-1, keepdims=True)
        along = jnp.mean(inner * std, axis=-1, keepdims=True)
        full = grads[rows].astype(F32) + (inner - mean - std * along) * inverse[rows]
        grad_out[rows] = full
        low_out[rows] = full.astype(BF16)
        return total + jnp.sum(grad * std, axis=0, keepdims=True)

    gain_out[...] = lax.fori_loop(0, 2, finish, jnp.zeros((1, resid.shape[1]), F32))
    moves[3].start()
    moves[4].start()
    give_ahead.wait_recv()

    def emit(i, carry):
        rows = at(i, step)
        rows_out[rows] = (resid[rows] + delta[rows] + ahead[rows] + ahead_in[rows].astype(F32)).astype(BF16)
        return carry

    lax.fori_loop(0, 2, emit, 0)
    moves[5].start()
    lax.fori_loop(0, 4, lambda s, carry: (combine(s), carry)[1], 0)
    for copy in (give_normed, give_grads, give_back, give_ahead):
        copy.wait_send()
    for s in range(4):
        for i in range(2):
            away_x(s, i).wait_send()
            away_y(s, i).wait_send()
            for copy in keep(s, i):
                copy.wait()
    for copy in moves[3:]:
        copy.wait()


def feed(resid, delta, upstream, masked, gain, w_in, w_in_far, w_out, w_far):
    own, features = resid.shape
    units = w_in.shape[2]
    dma = pltpu.SemaphoreType.DMA
    anywhere = pl.BlockSpec(memory_space=pl.ANY)
    whole = pl.BlockSpec(memory_space=pltpu.VMEM)

    def low(*shape):
        return pltpu.VMEM(shape, BF16)

    def high(*shape):
        return pltpu.VMEM(shape, F32)

    return pl.pallas_call(
        feed_kernel,
        in_specs=[anywhere] * 3 + [whole] * 2 + [anywhere] * 4,
        out_specs=[anywhere] * 5 + [whole],
        out_shape=[
            jax.ShapeDtypeStruct((2, 4, BLK, units), BF16),
            jax.ShapeDtypeStruct((2, 4, BLK, units), BF16),
            jax.ShapeDtypeStruct((own, features), F32),
            jax.ShapeDtypeStruct((own, features), BF16),
            jax.ShapeDtypeStruct((own, features), BF16),
            jax.ShapeDtypeStruct((1, features), F32),
        ],
        scratch_shapes=[
            high(own, features), high(own, features), low(own, features),
            high(own, features), low(own, features), low(own, features), dma((6,)),
            low(4, features, units), low(4, units, features), high(own, features), high(own, 1),
            low(2 * own, features), low(2 * own, features), low(features, 2 * own), low(features, 2 * own),
            low(2 * own, units), low(2 * own, units), low(4, features, units), low(4, features, units),
            high(2 * own, features), high(2 * own, features),
            low(own, features), low(own, features), low(own, features), low(own, features),
            low(2, 4, BLK, units), low(2, 4, BLK, units), high(2 * own, units),
            dma((9, 4)), dma((2, 2, 4)), dma((2,)), dma((2,)), dma((2,)), dma((2,)),
            dma((2, 4)), dma((2, 4)), dma((2, 4)), dma((2, 4)),
        ],
        compiler_params=pltpu.CompilerParams(
            collective_id=4, has_side_effects=True, vmem_limit_bytes=60 * 1024 * 1024
        ),
        cost_estimate=pl.CostEstimate(flops=26 * 10**9, transcendentals=2 * 10**6, bytes_accessed=10**8),
        name="feed",
    )(resid, delta, upstream, masked, gain, w_in, w_in_far, w_out, w_far)


def leave_kernel(
    scale,
    part_hbm, next_hbm, grad_hbm, out_hbm, joined_hbm, mixed_hbm, lhs_hbm, weight_hbm, std_hbm, time_hbm, feed_hbm, feed_in_hbm,
    totals, inverse_next, inverse, masked, gains, later_grad,
    space_qkv, space_out, feed_in_out, feed_out_out, time_qkv, time_out, rows_out, gains_out, embed_out,
    rows_in,
    part, std, base, w_out, dj, mixed, lhs, weight, low_grads, turned, dmixed, go,
    t_own, t_in, tz_out, tz_in, t_total, ty_out, ty_in, tc_out, tc_in,
    f_own, f_in, fz_out, fz_in, f_total, f_other, fc_out, fc_in,
    grads, a1_out, a1_in, b1_out, b1_in, a2_out, a2_in, b2_out, b2_in, z_out, z_in,
    half_out, half_in, ready, core_out, core_in, sums, sum_out, sum_in, share_in,
    a1_send, a1_recv, b1_send, b1_recv, a2_send, a2_recv, b2_send, b2_recv, z_send, z_recv,
    h_send, h_recv, r_send, r_recv, c_send, c_recv, s_send, s_recv, p_send, p_recv, local,
    g_send, g_recv, tx_send, tx_recv, tz_send, tz_recv, ty_send, ty_recv, fy_send, fy_recv, fz_send, fz_recv, t_local, f_local, fetched,
):
    y, x, c, z = (lax.axis_index(name) for name in AXES)
    near_y, near_x, pair = (1 - y, x, c, z), (y, 1 - x, c, z), (y, x, 1 - c, z)
    own = std.shape[0]
    third = go.shape[1] // 4
    wide = 3 * third
    two = 2 * third
    slab = 128

    fetches = [
        pltpu.make_async_copy(src, dst, fetched.at[i])
        for i, (src, dst) in enumerate((
            (part_hbm, part), (next_hbm, std), (grad_hbm, base), (out_hbm, w_out), (joined_hbm, dj), (mixed_hbm, mixed),
            (lhs_hbm, lhs), (weight_hbm, weight), (feed_in_hbm, f_other),
        ))
    ]
    for copy in fetches:
        copy.start()
    fetch_std = pltpu.make_async_copy(std_hbm, std, fetched.at[9])

    barrier = pltpu.get_barrier_semaphore()
    for dc in range(2):
        for dz in range(4):
            if dc or dz:
                pl.semaphore_signal(barrier, inc=1, device_id=(y, x, (c + dc) % 2, (z + dz) % 4), device_id_type=MESH)
    for peer in (near_y, near_x):
        pl.semaphore_signal(barrier, inc=1, device_id=peer, device_id_type=MESH)
    pl.semaphore_wait(barrier, 9)

    def remote(src, dst, send, recv, peer):
        return pltpu.make_async_remote_copy(
            src_ref=src, dst_ref=dst, send_sem=send, recv_sem=recv, device_id=peer, device_id_type=MESH
        )

    def at(i, length):
        return pl.ds(pl.multiple_of(i * length, length), length)

    def along(r):
        return (y, x, c, (z + r) % 4)

    def time_x(yb):
        return remote(time_hbm.at[at(2 * yb + 1 - x, BLK)], t_in.at[yb], tx_send.at[yb], tx_recv.at[yb], near_x)

    def time_keep(yb):
        return pltpu.make_async_copy(time_hbm.at[at(2 * yb + x, BLK)], t_own.at[yb], t_local.at[yb])

    def time_z(r):
        return remote(tz_out.at[r], tz_in.at[r], tz_send.at[r], tz_recv.at[r], along(1))

    def feed_y(r):
        s = (z + r) % 4
        return remote(feed_hbm.at[1 - y, s], f_in.at[r], fy_send.at[r], fy_recv.at[r], near_y)

    def feed_keep(r):
        return pltpu.make_async_copy(feed_hbm.at[y, (z + r) % 4], f_own.at[r], f_local.at[r])

    def feed_z(r):
        return remote(fz_out.at[r], fz_in.at[r], fz_send.at[r], fz_recv.at[r], along(1))

    for r in (3, 2, 1, 0):
        feed_y(r).start()
        feed_keep(r).start()
    for yb in range(2):
        time_x(yb).start()
        time_keep(yb).start()

    def feed_step(t):
        r = 3 - t
        feed_y(r).wait_recv()
        feed_keep(r).wait()
        total = f_own[r].astype(F32) + f_in[r].astype(F32)
        if t > 0:
            feed_z(t - 1).wait_recv()
            total = total + fz_in[t - 1].astype(F32)
        if t == 3:
            f_total[...] = total
        else:
            fz_out[t] = total.astype(BF16)
            feed_z(t).start()

    def time_step(t):
        if t == 0:
            for yb in range(2):
                time_x(yb).wait_recv()
                time_keep(yb).wait()
        else:
            time_z(t - 1).wait_recv()
        piece_at = at((z + 3 - t) % 4, BLK)
        for yb in range(2):
            total = t_own[yb, :, piece_at].astype(F32) + t_in[yb, :, piece_at].astype(F32)
            if t > 0:
                total = total + tz_in[t - 1, yb].astype(F32)
            if t == 3:
                t_total[yb] = total
            else:
                tz_out[t, yb] = total.astype(BF16)
        if t < 3:
            time_z(t).start()

    step = own // 2
    for copy in fetches[:3]:
        copy.wait()

    def norm_back(grad, standard, weights, inv):
        inner = grad * weights
        mean = jnp.mean(inner, axis=-1, keepdims=True)
        slope = jnp.mean(inner * standard, axis=-1, keepdims=True)
        return (inner - mean - standard * slope) * inv

    def after_time(i, total):
        rows = at(i, step)
        grad, standard = part[rows], std[rows]
        full = base[rows] + norm_back(grad, standard, gains[2:3], inverse_next[rows])
        base[rows] = full
        low_grads[rows] = full.astype(BF16)
        return total + jnp.sum(grad * standard, axis=0, keepdims=True)

    zero = jnp.zeros((1, std.shape[1]), F32)
    next_grad = lax.fori_loop(0, 2, after_time, zero)
    give = remote(low_grads.at[pl.ds(0, own)], low_grads.at[pl.ds(own, own)], g_send.at[0], g_recv.at[0], pair)
    give.start()
    fetch_std.start()
    for copy in fetches[3:6]:
        copy.wait()

    def attend(i, carry):
        rows = at(i, slab)
        for h in range(mixed.shape[1] // PAIR):
            places = [pl.ds((3 * h + j) * PAIR, PAIR) for j in range(3)]
            q, k, v = (dj[rows, place] for place in places)
            lines = [totals[i, 2 * h + j : 2 * h + j + 1, :] for j in range(2)]
            found = attend_pair_back(q, k, v, dmixed[rows, h * PAIR : (h + 1) * PAIR], lines, None, scale)
            for place, value in zip(places, found):
                dj[rows, place] = value.astype(BF16)
        return carry

    def turn(i, carry):
        turned[:, at(i, slab)] = low_grads[at(i, slab)].T
        return carry

    def attend_half(t, *between):
        rows = pl.ds(t * own, own)
        first, count = t * own // slab, own // slab
        dmixed[rows] = dot_nt(low_grads[rows], w_out[...]).astype(BF16)
        between[0]()
        lax.fori_loop(first, first + count // 2, attend, 0)
        between[1]()
        lax.fori_loop(first + count // 2, first + count, attend, 0)
        between[2]()
        lax.fori_loop(first, first + count, turn, 0)

    def nothing():
        pass

    attend_half(0, lambda: feed_step(0), nothing, lambda: feed_step(1))
    give.wait_recv()
    attend_half(1, nothing, lambda: feed_step(2), lambda: time_step(0))
    for copy in fetches[6:]:
        copy.wait()
    def away(i, carry):
        rows = pl.ds(pl.multiple_of(own + i * step, step), step)
        half_out[pl.ds(pl.multiple_of(i * step, step), step)] = dot_nt(dj[rows], weight[...]).astype(BF16)
        return carry

    lax.fori_loop(0, 2, away, 0)
    swap = remote(half_out, half_in, h_send.at[0], h_recv.at[0], pair)
    swap.start()

    def block(yb, xb):
        return pl.ds(pl.multiple_of(BLK * (2 * yb + xb), BLK), BLK)

    def a1(i):
        return remote(a1_out.at[i], a1_in.at[i], a1_send.at[i], a1_recv.at[i], near_x)

    def b1(i):
        return remote(b1_out.at[i], b1_in.at[i], b1_send.at[i], b1_recv.at[i], near_y)

    def a2(i):
        return remote(a2_out.at[i], a2_in.at[i], a2_send.at[i], a2_recv.at[i], near_y)

    def b2(i):
        return remote(b2_out.at[i], b2_in.at[i], b2_send.at[i], b2_recv.at[i], near_x)

    def to_z(r):
        return remote(z_out.at[r], z_in.at[r], z_send.at[r], z_recv.at[r], along(r))

    def send_first(i):
        a1(i).start()
        b1(i).start()

    def piece(i, carry):
        s = (z + i + 1) % 4
        made = dot_nn(lhs[...], dj[:, pl.ds(pl.multiple_of(s * wide, third), wide)])
        grads[i, :, :wide] = made
        grads[i, :, wide:] = go[:, pl.ds(pl.multiple_of(s * third, third), third)].astype(F32)
        for b in range(2):
            a1_out[i, b] = grads[i, block(b, 1 - x), :two].astype(BF16)
            b1_out[i, b] = grads[i, block(1 - y, b), two:].astype(BF16)
        pl.when(i < 2)(lambda: send_first(i))
        return carry


    def second(i):
        a1(i).wait_recv()
        a2_out[i] = (grads[i, block(1 - y, x), :two] + a1_in[i, 1 - y].astype(F32)).astype(BF16)
        a2(i).start()
        b1(i).wait_recv()
        b2_out[i] = (grads[i, block(y, 1 - x), two:] + b1_in[i, 1 - x].astype(F32)).astype(BF16)
        b2(i).start()
        grads[i, block(y, x), :two] = grads[i, block(y, x), :two] + a1_in[i, y].astype(F32)
        grads[i, block(y, x), two:] = grads[i, block(y, x), two:] + b1_in[i, x].astype(F32)

    def third_step(i):
        a2(i).wait_recv()
        b2(i).wait_recv()
        grads[i, block(y, x), :two] = grads[i, block(y, x), :two] + a2_in[i].astype(F32)
        grads[i, block(y, x), two:] = grads[i, block(y, x), two:] + b2_in[i].astype(F32)
        if i < 3:
            z_out[i + 1] = grads[i, block(y, x), :].astype(BF16)
            to_z(i + 1).start()

    fetch_std.wait()
    sums[...] = jnp.zeros_like(sums)
    sums[1:2] = next_grad
    sums[2:3] = later_grad[...]
    swap.wait_recv()

    def home(i, totals):
        rows = pl.ds(pl.multiple_of(i * step, step), step)
        grad = dot_nt(dj[rows], weight[...]) + half_in[rows].astype(F32)
        standard = std[rows]
        full = base[rows] + norm_back(grad, standard, gains[1:2], inverse[rows])
        hide = masked[rows] > 0.0
        ready[rows] = jnp.where(hide, 0.0, full).astype(BF16)
        return (
            totals[0] + jnp.sum(grad * standard, axis=0, keepdims=True),
            totals[1] + jnp.sum(jnp.where(hide, full, 0.0), axis=0, keepdims=True),
        )

    gain_grad, embed_grad = lax.fori_loop(0, 2, home, (zero, zero))
    sums[0:1] = gain_grad
    sums[3:4] = embed_grad

    def columns(s):
        return pl.ds(pl.multiple_of(s * BLK, BLK), BLK)

    def stays(k):
        return jnp.logical_and(z == k, z // 2 == c)

    def ride(k):
        slot = 2 * (z % 2) + c
        return remote(ready.at[:, columns(k)], rows_in.at[slot], r_send.at[k], r_recv.at[slot], (y, x, z // 2, k))

    def ride_local(k):
        return pltpu.make_async_copy(ready.at[:, columns(k)], rows_in.at[2 * (z % 2) + c], local.at[3])

    for k in range(4):
        pl.when(stays(k))(lambda k=k: ride_local(k).start())
        pl.when(jnp.logical_not(stays(k)))(lambda k=k: ride(k).start())
    time_step(1)
    go[...] = dot_nn(turned[...], mixed[...]).astype(BF16)
    lax.fori_loop(0, 4, piece, 0)

    def share(h):
        peer = (pair, near_y, near_x)[h]
        return remote(sum_out.at[h], sum_in.at[h], s_send.at[h], s_recv.at[h], peer)

    def begin_share(h):
        sum_out[h] = sums[...]
        share(h).start()

    def end_share(h):
        share(h).wait_recv()
        sums[...] = sums[...] + sum_in[h]

    begin_share(0)
    second(0)
    send_first(2)
    time_step(2)
    second(1)
    send_first(3)
    third_step(0)
    end_share(0)
    begin_share(1)
    second(2)
    third_step(1)
    end_share(1)
    begin_share(2)
    second(3)
    third_step(2)
    end_share(2)
    sum_out[3] = sums[...]

    def deal(r):
        s = (z + r) % 4
        return remote(sum_out.at[3, :, columns(s)], share_in.at[r], p_send.at[r], p_recv.at[r], (y, x, c, s))

    for r in (1, 2, 3):
        deal(r).start()
    third_step(3)
    parity = BLK // 2

    time_step(3)
    ty_out[...] = t_total[1 - y].astype(BF16)
    swap_y = remote(ty_out, ty_in, ty_send.at[0], ty_recv.at[0], near_y)
    swap_y.start()
    feed_step(3)
    fc_out[0] = f_other[at(1 - c, parity)].astype(BF16)
    fc_out[1] = f_total[at(1 - c, parity)].astype(BF16)
    swap_feed = remote(fc_out, fc_in, c_send.at[1], c_recv.at[1], pair)
    swap_feed.start()
    units = f_total.shape[1]
    feed_in_out[:, at(c, units)] = f_other[at(c, parity)]
    feed_out_out[at(c, units)] = f_total[at(c, parity)].T
    swap_y.wait_recv()
    tc_out[0] = t_total[y, at(1 - c, parity)].astype(BF16)
    tc_out[1] = ty_in[at(1 - c, parity)]
    swap_time = remote(tc_out, tc_in, c_send.at[2], c_recv.at[2], pair)
    swap_time.start()
    for k in range(4):
        pl.when(stays(k))(lambda k=k: ride_local(k).wait())
        from_self = jnp.logical_and(2 * c + k // 2 == z, c == k % 2)

        def landed(k=k):
            remote(ready.at[:, columns(k)], rows_in.at[k], r_send.at[k], r_recv.at[k], near_y).wait_recv()

        pl.when(jnp.logical_not(from_self))(landed)
    rows_out[...] = rows_in[...].astype(F32)
    for r in (1, 2, 3):
        to_z(r).wait_recv()
    total = grads[3, block(y, x), :]
    for r in (1, 2, 3):
        total = total + z_in[r].astype(F32)
    grads[3, block(y, x), :] = total
    rows = BLK // 2

    def core_rows(core):
        return pl.ds(pl.multiple_of(BLK * (2 * y + x) + rows * core, rows), rows)

    core_out[...] = grads[3, core_rows(1 - c), :].astype(BF16)
    last = remote(core_out, core_in, c_send.at[0], c_recv.at[0], pair)
    last.start()
    def place(core, value):
        for j in range(3):
            space_qkv[j, :, at(core, third)] = value[:, j * third : (j + 1) * third]
        space_out[at(core, third)] = value[:, 3 * third :].T

    place(c, grads[3, core_rows(c), :])
    result = sums[:, columns(z)]
    for r in (1, 2, 3):
        deal(r).wait_recv()
        result = result + share_in[r]
    gains_out[...] = result[:3]
    embed_out[...] = result[3:4]
    swap_feed.wait_recv()
    feed_in_out[:, at(1 - c, units)] = fc_in[0].astype(F32)
    feed_out_out[at(1 - c, units)] = fc_in[1].astype(F32).T
    swap_time.wait_recv()
    mine = (t_total[y, at(c, parity)], ty_in[at(c, parity)].astype(F32))
    other = (tc_in[0].astype(F32), tc_in[1].astype(F32))
    by_head = []
    for yb in range(2):
        for cb in range(2):
            by_head.append(
                jnp.where(
                    c == cb,
                    jnp.where(y == yb, mine[0], mine[1]),
                    jnp.where(y == yb, other[0], other[1]),
                )
            )
    for j in range(4):
        made = jnp.concatenate([v[:, j * HEAD_DIM : (j + 1) * HEAD_DIM] for v in by_head], axis=1)
        if j < 3:
            time_qkv[j] = made
        else:
            time_out[...] = made.T
    last.wait_recv()
    place(1 - c, core_in[...].astype(F32))

    for copy in (last, swap, give, swap_y, swap_feed, swap_time):
        copy.wait_send()
    for yb in range(2):
        time_x(yb).wait_send()
    for r in range(4):
        feed_y(r).wait_send()
    for t in range(3):
        time_z(t).wait_send()
        feed_z(t).wait_send()
    for i in range(4):
        for copy in (a1(i), b1(i), a2(i), b2(i)):
            copy.wait_send()
    for r in (1, 2, 3):
        to_z(r).wait_send()
        deal(r).wait_send()
    for h in range(3):
        share(h).wait_send()
    for k in range(4):
        pl.when(jnp.logical_not(stays(k)))(lambda k=k: ride(k).wait_send())


def leave(
    part, std_next, grad, w_out, joined, mixed, lhs, weight, std, g_time, g_out, g_in,
    totals, inverse_next, inverse, masked, gains, later_grad, scale,
):
    own, features = std.shape
    cols4 = mixed.shape[1]
    quarter = cols4 // 4
    units = g_in.shape[1]
    dma = pltpu.SemaphoreType.DMA
    anywhere = pl.BlockSpec(memory_space=pl.ANY)
    whole = pl.BlockSpec(memory_space=pltpu.VMEM)
    parity = BLK // 2

    def low(*shape):
        return pltpu.VMEM(shape, BF16)

    def high(*shape):
        return pltpu.VMEM(shape, F32)

    return pl.pallas_call(
        functools.partial(leave_kernel, scale),
        in_specs=[anywhere] * 12 + [whole] * 6,
        out_specs=[whole] * 9,
        out_shape=[
            jax.ShapeDtypeStruct(shape, F32)
            for shape in (
                (3, parity, 2 * quarter), (2 * quarter, parity), (parity, 2 * units), (2 * units, parity),
                (3, parity, BLK), (BLK, parity), (4, own, BLK), (3, BLK), (1, BLK),
            )
        ],
        scratch_shapes=[
            low(4, own, BLK),
            high(own, features), high(own, features), high(own, features), low(*w_out.shape), low(*joined.shape),
            low(*mixed.shape), low(*lhs.shape), low(*weight.shape), low(2 * own, features), low(features, 2 * own),
            low(*mixed.shape), low(features, cols4),
            low(2, BLK, features), low(2, BLK, features), low(4, 2, BLK, BLK), low(4, 2, BLK, BLK), high(2, BLK, BLK),
            low(BLK, BLK), low(BLK, BLK), low(2, parity, BLK), low(2, parity, BLK),
            low(4, BLK, units), low(4, BLK, units), low(4, BLK, units), low(4, BLK, units),
            high(BLK, units), high(BLK, units), low(2, parity, units), low(2, parity, units),
            high(4, features, cols4),
            low(4, 2, BLK, 2 * quarter), low(4, 2, BLK, 2 * quarter), low(4, 2, BLK, 2 * quarter), low(4, 2, BLK, 2 * quarter),
            low(4, BLK, 2 * quarter), low(4, BLK, 2 * quarter), low(4, BLK, 2 * quarter), low(4, BLK, 2 * quarter),
            low(4, BLK, cols4), low(4, BLK, cols4),
            low(own, features), low(own, features), low(own, features),
            low(parity, cols4), low(parity, cols4),
            high(8, features), high(4, 8, features), high(3, 8, features), high(4, 8, BLK),
        ]
        + [dma((4,))] * 10
        + [dma((1,)), dma((1,)), dma((4,)), dma((4,)), dma((3,)), dma((3,)), dma((3,)), dma((3,)), dma((4,)), dma((4,)), dma((4,))]
        + [dma((1,)), dma((1,)), dma((2,)), dma((2,)), dma((4,)), dma((4,)), dma((1,)), dma((1,))]
        + [dma((4,)), dma((4,)), dma((4,)), dma((4,)), dma((2,)), dma((4,)), dma((10,))],
        compiler_params=pltpu.CompilerParams(
            collective_id=3, has_side_effects=True, vmem_limit_bytes=62 * 1024 * 1024
        ),
        cost_estimate=pl.CostEstimate(flops=2 * 10**10, transcendentals=10**6, bytes_accessed=10**8),
        name="leave",
    )(
        part, std_next, grad, w_out, joined, mixed, lhs, weight, std, g_time, g_out, g_in,
        totals, inverse_next, inverse, masked, gains, later_grad,
    )


def tie(*values):
    return lax.optimization_barrier(values)


def norm_rows(resid):
    mean = jnp.mean(resid, axis=-1, keepdims=True)
    centered = resid - mean
    inverse = lax.rsqrt(jnp.mean(centered * centered, axis=-1, keepdims=True) + eps_norm)
    return (centered * inverse, inverse)


def norm_rows_back(grad, standardized, inverse, gain):
    gain_grad = jnp.sum(grad * standardized, axis=0)
    inner = grad * gain
    mean = jnp.mean(inner, axis=-1, keepdims=True)
    along = jnp.mean(inner * standardized, axis=-1, keepdims=True)
    return ((inner - mean - standardized * along) * inverse, gain_grad)


def cols(parts):
    return jnp.concatenate(parts, axis=1)


def rows_of(parts):
    return jnp.concatenate(parts, axis=0)


def token_parallel(
    tokens,
    cotangent,
    ratio,
    priority,
    frame_order,
    mask_embed,
    gains,
    qkv_space,
    out_space,
    qkv_time,
    out_time,
    w_in,
    w_out,
):
    scale = 1.0 / math.sqrt(HEAD_DIM)
    y, x, c, z = (lax.axis_index(name) for name in AXES)
    patches = tokens.shape[2]
    width = qkv_space.shape[0]
    frames_own = tokens.shape[0] * tokens.shape[1] // 4
    frames_all = frame_order.shape[1]
    own = frames_own * patches
    hidden_own = w_in.shape[1] // 2
    plane = 2 * y + x
    k_own = 2 * (z % 2) + c

    masked_here = (priority < ratio[:, None, None]).astype(jnp.int32).reshape(2, -1)
    info = cols([masked_here, frame_order])
    info = jnp.where(z // 2 == c, info, hop_c(info))
    info = lax.dynamic_index_in_dim(info, z % 2, 0, keepdims=False)
    masked = lax.dynamic_slice_in_dim(info, c * own, own, 0)[:, None] != 0
    order = info[2 * own :].reshape(2, 2, frames_own)
    order = jnp.where(y == 1, order[::-1], order)
    order = jnp.where(c == 1, order[:, ::-1], order).swapaxes(0, 1).reshape(frames_all)
    order = jnp.repeat(order, GROUP)
    patch = jnp.arange(frames_all * GROUP) % GROUP
    visible = (order[:, None] <= order[None, :]) & (patch[:, None] == patch[None, :])
    bias = jnp.where(visible, 0.0, -1e30).astype(F32)

    vectors = rows_of([mask_embed[None], gains, jnp.zeros((4, BLK), BF16)])
    (
        ws_qkv, ws_out, wt_all, wf_out, wf_in, joined0, turned0, std0,
        mixed0, total0, inv0, resid1, std1, inv1, normed1, vectors,
    ) = enter(
        tokens.reshape(4, own, BLK),
        vectors,
        jnp.swapaxes(qkv_space, 0, 1),
        out_space,
        jnp.swapaxes(qkv_time, 0, 1),
        out_time,
        w_out,
        w_in,
        masked.astype(F32),
        scale,
    )

    half = qkv_space.shape[2] // 2
    turned1, joined1, mixed1, total1, delta, upstream, wf_far, wf_in_far = time_call(
        False,
        normed1.reshape(frames_own, patches, width),
        cotangent.reshape(4, own, BLK),
        [wf_out, wf_in],
        wt_all,
        bias,
        scale,
    )
    w_in_half, w_out_half, grad2, grad2_low, block_rows, gain_grad2 = feed(
        resid1, delta.reshape(own, width), upstream, masked.astype(F32), vectors, wf_in, wf_in_far, wf_out, wf_far
    )

    part1, g_time, g_w_in, block_out = time_call(
        True,
        grad2_low.reshape(frames_own, patches, width),
        block_rows,
        [joined1, total1, w_in_half, turned1, mixed1],
        wt_all,
        bias,
        scale,
    )
    block_out = block_out.reshape(tokens.shape)
    grad_qkv_space, grad_out_space, grad_w_in, grad_w_out, grad_qkv_time, grad_out_time, grad_tokens, grad_gains, grad_embed = leave(
        part1.reshape(own, width), std1, grad2, ws_out, joined0, mixed0, turned0, ws_qkv, std0, g_time, w_out_half, g_w_in,
        total0, inv1, inv0, masked.astype(F32), vectors, gain_grad2, scale,
    )
    return (
        block_out,
        grad_tokens.reshape(tokens.shape),
        grad_embed.reshape(BLK),
        grad_gains,
        jnp.swapaxes(grad_qkv_space, 0, 1),
        grad_out_space,
        jnp.swapaxes(grad_qkv_time, 0, 1),
        grad_out_time,
        grad_w_in,
        grad_w_out,
    )


def solution(mesh):
    sizes = (mesh.shape["tm"], mesh.shape["clip"], mesh.shape["mp"])
    if sizes == (2, 4, 4):
        mesh = jax.sharding.Mesh(mesh.devices.reshape(2, 2, 2, 4), AXES)
        step, clip = token_parallel, ("x", "c")
    else:
        step, clip = shards, ("clip",)
    return jax.shard_map(
        step,
        mesh=mesh,
        in_specs=(
            P(clip, "tm", None, "mp"),
            P(clip, "tm", None, "mp"),
            P(clip),
            P(clip, "tm", None),
            P(clip, None),
            P("mp"),
            P(None, "mp"),
            P(None, None, "mp"),
            P("mp", None),
            P(None, None, "mp"),
            P("mp", None),
            P(None, "mp"),
            P("mp", None),
        ),
        out_specs=(
            P(clip, "tm", None, "mp"),
            P(clip, "tm", None, "mp"),
            P("mp"),
            P(None, "mp"),
            P(("tm",) + clip, None, "mp"),
            P("mp", ("tm",) + clip),
            P(("tm",) + clip, None, "mp"),
            P("mp", ("tm",) + clip),
            P(("tm",) + clip, "mp"),
            P("mp", ("tm",) + clip),
        ),
        check_vma=False,
    )
```

profile of v0, /device:TPU:9, one launch (start us, length us, event | category | flops | bytes accessed | tf_op | source)
XLA Modules:
  0.0 395.7 jit_solution(14750083085465025683)
XLA Ops:
  0.6 0.8 convert_bitcast_fusion
  1.4 0.7 constant_dynamic-update-slice_fusion
  2.1 0.7 collective-permute-start
  2.8 0.7 broadcast_in_dim.21
  3.4 0.1 pad.2.clone
  3.5 1.3 maximum_maximum_fusion.vec
  4.9 0.0 collective-permute-done
  4.9 0.1 dynamic-slice_reduce_fusion
  5.0 0.1 reshape.109
  5.1 0.1 reshape.110
  5.2 0.1 broadcast_in_dim.23
  5.3 0.1 le.15
  5.4 0.1 fusion
  5.5 0.9 copy.24.masked
  6.3 0.7 and_select_fusion.refs_5_.refs_8_
  7.1 103.8 %enter.1 = (bf16[1024,1536]{1,0:T(8,128)(2,1)}, bf16[512,1024]{1,0:T(8,128)(2,1)}, bf16[1024,1024]{1,0:T(8,128)(2,1)}, bf16[4,512,1024]{2,1,0:T(8,128)(2,1)}, bf...) custom-call(bf16[4,512,256]{2,1,0:T(8,128)(2,1)} %bitcast.28, ...), custom_call_target="tpu_custom_call" | custom-call | flops 10000000000 | bytes 100000000 | tf_op jit(solution)/shard_map/enter/pallas_call | solution.py:909
  110.8 57.7 %time_forward.1 = (bf16[8,1024,256]{2,1,0:T(8,128)(2,1)}, bf16[16,128,768]{2,1,0:T(8,128)(2,1)}, bf16[16,128,256]{2,1,0:T(8,128)(2,1)}, f32[16,4,128]{2,1,0:T(4,...) custom-call(bf16[4,128,1024]{2,1,0:T(8,128)(2,1)} %bitcast.32, ...), custom_call_target="tpu_custom_call" | custom-call | flops 10000000000 | bytes 100000000 | tf_op jit(solution)/shard_map/time_forward/pallas_call | solution.py:1282
  168.6 63.4 %feed.1 = (bf16[2,4,256,512]{3,2,1,0:T(8,128)(2,1)}, bf16[2,4,256,512]{3,2,1,0:T(8,128)(2,1)}, f32[512,1024]{1,0:T(8,128)}, bf16[512,1024]{1,0:T(8,128)(2,1)}, b...) custom-call(f32[512,1024]{1,0:T(8,128)} %get-tuple-element.53.resid_hbm, f32[512,1024]{1,0:T(8,128)} %bitcast.31, ...), custom_call_target="tpu_custom_call" | custom-call | flops 25999998976 | bytes 100000000 | tf_op jit(solution)/shard_map/feed/pallas_call | solution.py:1533
  232.0 54.0 %time_back.1 = (f32[4,128,1024]{2,1,0:T(8,128)}, bf16[1024,1024]{1,0:T(8,128)(2,1)}, f32[256,512]{1,0:T(8,128)}, bf16[4,512,256]{2,1,0:T(8,128)(2,1)}) custom-call(bf16[4,128,1024]{2,1,0:T(8,128)(2,1)} %bitcast.33, bf16[512,1024]{1,0:T(8,128)(2,1)} %get-tuple-element.64.refs_1_, bf16[16,128,768]{2,1,0:T(8,128)(2,1)} %get-tuple-element.65.refs_2_, ...), custom_call_target="tpu_custom_call" | custom-call | flops 10000000000 | bytes 100000000 | tf_op jit(solution)/shard_map/time_back/pallas_call | solution.py:1282
  286.0 0.0 copy-start.1
  286.0 100.7 %leave.1 = (f32[3,128,256]{2,1,0:T(8,128)}, f32[256,128]{1,0:T(8,128)}, f32[128,1024]{1,0:T(8,128)}, f32[1024,128]{1,0:T(8,128)}, f32[3,128,256]{2,1,0:T(8,128)}...) custom-call(f32[512,1024]{1,0:T(8,128)} %bitcast.30, ...), custom_call_target="tpu_custom_call" | custom-call | flops 20000000000 | bytes 100000000 | tf_op jit(solution)/shard_map/leave/pallas_call | solution.py:1998
  386.8 0.0 copy-start
  386.8 0.0 copy-done.1
  386.8 1.0 copy.41
  387.8 1.0 copy-done
  388.7 0.0 copy-start.9
  388.7 0.0 copy-start.8
  388.8 0.0 copy-start.5
  388.8 0.0 copy-start.7
  388.8 0.0 copy-start.4
  388.8 0.0 copy-start.6
  388.8 1.3 copy.42
  390.1 0.0 copy-done.9
  390.1 0.6 copy.43
  390.7 0.0 copy-done.8
  390.7 0.6 copy.44
  391.3 0.0 copy-done.5
  391.3 0.7 copy.45
  392.0 0.0 copy-done.7
  392.0 0.7 copy.46
  392.7 0.0 copy-done.4
  392.7 0.7 copy.47
  393.4 0.0 copy-done.6
  393.4 0.7 copy.48
  394.1 0.0 copy-done.3
  394.1 0.8 copy.49
  394.9 0.0 copy-done.2
  394.9 0.8 copy.50
  (10 shorter events, 0.1 us)
Async XLA Ops:
  2.1 2.8 collective-permute-start
  286.0 100.8 %copy-start.1 = (bf16[4,512,256]{2,1,0:T(8,128)(2,1)S(1)}, bf16[4,512,256]{2,1,0:T(8,128)(2,1)}, u32[]{:S(2)}) copy-start(bf16[4,512,256]{2,1,0:T(8,128)(2,1)} %get-tuple-element.70) | copy-start | bytes 3145732
  386.8 2.0 copy-start
  388.7 1.4 copy-start.9
  388.7 1.9 copy-start.8
  388.8 2.5 copy-start.5
  388.8 3.3 copy-start.7
  388.8 3.9 copy-start.4
  388.8 4.7 %copy-start.6 = (f32[256,128]{1,0:T(8,128)S(1)}, f32[256,128]{1,0:T(8,128)}, u32[]{:S(2)}) copy-start(f32[256,128]{1,0:T(8,128)} %get-tuple-element.113) | copy-start | bytes 393220
  390.1 4.0 %copy-start.3 = (f32[128,1024]{1,0:T(8,128)S(1)}, f32[128,1024]{1,0:T(8,128)}, u32[]{:S(2)}) copy-start(f32[128,1024]{1,0:T(8,128)} %get-tuple-element.114) | copy-start | bytes 1572868
  390.1 4.8 %copy-start.2 = (f32[1024,128]{1,0:T(8,128)S(1)}, f32[1024,128]{1,0:T(8,128)}, u32[]{:S(2)}) copy-start(f32[1024,128]{1,0:T(8,128)} %get-tuple-element.115) | copy-start | bytes 1572868
where the time goes:
time: 397 us; the launch traced here: 396 us
  Pallas kernels  380 us (96%)
  local copies, waits for them, and re-layouts  11.6 us (3%)
    pallas_call x2, Pallas kernels, time_call(): pl.pallas_call(functools.partial(time_kernel, back, scale, heads), in_spe...  112 us
    pallas_call x1, Pallas kernels, enter(): pl.pallas_call(functools.partial(enter_kernel, scale), in_specs=[anywhere...  104 us
    pallas_call x1, Pallas kernels, leave(): pl.pallas_call(functools.partial(leave_kernel, scale), in_specs=[anywhere...  101 us
    pallas_call x1, Pallas kernels, feed(): pl.pallas_call(feed_kernel, in_specs=[anywhere] * 3 + [whole] * 2 + [anyw...  63.4 us
    unnamed x31, local copies, waits for them, and re-layouts  8.86 us
  transfers between devices with their start and end apart: 1, of which 0 were waited for; matrix products, arithmetic and copies ran while one was open for 1% of the time, Pallas kernels for 0%

commit v1 on v0

--- a/solution.py
+++ b/solution.py
@@ -943,9 +943,9 @@
         refs = refs[13:-17]
     else:
         (own_ref, rider_ref, far_ref, in_ref, wt_hbm, bias_ref) = refs[:6]
-        (turned_ref, out_ref, mixed_ref, total_ref, delta_ref, rider_out, spread_out, in_out) = refs[6:14]
-        (turned, wt_ref, load_sem) = refs[-3:]
-        refs = refs[14:-3]
+        (turned_ref, out_hbm, mixed_hbm, total_ref, delta_ref, rider_out, spread_out, in_out) = refs[6:14]
+        (turned, wt_ref, out_ref, mixed_ref, load_sem, keep_sem) = refs[-6:]
+        refs = refs[14:-6]
     (
         wq_ref, wo_ref, held, wide, narrow, kept, core_out, core_in, near_out, near_in,
         gy_send, gy_recv, gc_send, gc_recv, gd_send, gd_recv, sc_send, sc_recv, sy_send, sy_recv,
@@ -998,6 +998,12 @@
 
     def scatter_y(k):
         return remote(near_out.at[k], near_in.at[k], sy_send.at[k], sy_recv.at[k], near)
+
+    def save_results(k):
+        return [
+            pltpu.make_async_copy(src.at[:, patches(k)], dst.at[:, patches(k)], keep_sem.at[i, k])
+            for i, (src, dst) in enumerate(((out_ref, out_hbm), (mixed_ref, mixed_hbm)))
+        ]
 
     def save(k):
         there = (turned_ref.at[k], turned.at[k]) if back else (turned.at[k], turned_ref.at[k])
@@ -1183,6 +1189,8 @@
                 slab = held[b * frames : (b + 1) * frames, patches(k)].reshape(frames * CHUNK, held.shape[2])
                 turned[k, :, b * frames * CHUNK : (b + 1) * frames * CHUNK] = slab.T
             save(k).start()
+            for copy in save_results(k):
+                copy.start()
         if back:
             pl.when(k == chunks // 2 - 1)(halve)
         return carry
@@ -1231,6 +1239,8 @@
             copy.wait_send()
         if not back:
             save(k).wait()
+            for copy in save_results(k):
+                copy.wait()
     if not back:
         for i in range(6):
             spread_x(i, 1).wait_recv()
@@ -1284,7 +1294,7 @@
         in_specs=[anywhere] * 2
         + ([anywhere, whole, anywhere, anywhere, anywhere] if back else [anywhere] * 2)
         + [anywhere, whole],
-        out_specs=([] if back else [anywhere]) + [whole] * (len(out_shape) - held + back) + [anywhere] * (held - 1),
+        out_specs=([] if back else [anywhere] * 3) + [whole] * (3 if back else 2) + [anywhere] * (held - 1),
         out_shape=out_shape,
         scratch_shapes=[
             pltpu.VMEM((features, 3 * width), BF16),
@@ -1307,7 +1317,9 @@
         + ([pltpu.VMEM((features, 3 * width), F32), pltpu.VMEM((width, features), F32)] if back else [])
         + [pltpu.VMEM(weights.shape, BF16)]
         + ([pltpu.VMEM(saved[0].shape, BF16), pltpu.VMEM(saved[4].shape, BF16)] if back else [])
-        + [dma((4,))],
+        + ([] if back else [pltpu.VMEM(out_shape[1].shape, BF16), pltpu.VMEM(out_shape[2].shape, BF16)])
+        + [dma((4,))]
+        + ([] if back else [dma((2, chunks))]),
         compiler_params=pltpu.CompilerParams(
             collective_id=2 if back else 1, has_side_effects=True, vmem_limit_bytes=60 * 1024 * 1024
         ),

time: 397 us -> 396 us (level)
  no operation moved by 1% of the time
where the time goes in v1:
time: 396 us; the launch traced here: 394 us
  Pallas kernels  378 us (95%)
  local copies, waits for them, and re-layouts  11.6 us (3%)
    pallas_call x2, Pallas kernels, time_call(): pl.pallas_call(functools.partial(time_kernel, back, scale, heads), in_spe...  111 us
    pallas_call x1, Pallas kernels, enter(): pl.pallas_call(functools.partial(enter_kernel, scale), in_specs=[anywhere...  104 us
    pallas_call x1, Pallas kernels, leave(): pl.pallas_call(functools.partial(leave_kernel, scale), in_specs=[anywhere...  101 us
    pallas_call x1, Pallas kernels, feed(): pl.pallas_call(feed_kernel, in_specs=[anywhere] * 3 + [whole] * 2 + [anyw...  63.4 us
    unnamed x31, local copies, waits for them, and re-layouts  8.86 us
  transfers between devices with their start and end apart: 1, of which 0 were waited for; matrix products, arithmetic and copies ran while one was open for 1% of the time, Pallas kernels for 0%

profile of v1, /device:TPU:9, one launch (start us, length us, event | category | flops | bytes accessed | tf_op | source)
XLA Modules:
  0.0 394.5 jit_solution(13998611973219423102)
XLA Ops:
  0.6 0.8 convert_bitcast_fusion
  1.4 0.7 constant_dynamic-update-slice_fusion
  2.1 0.7 collective-permute-start
  2.8 0.7 broadcast_in_dim.21
  3.4 0.1 pad.2.clone
  3.5 1.3 maximum_maximum_fusion.vec
  4.9 0.0 collective-permute-done
  4.9 0.1 dynamic-slice_reduce_fusion
  5.0 0.1 reshape.109
  5.1 0.1 reshape.110
  5.2 0.1 broadcast_in_dim.23
  5.3 0.1 le.15
  5.4 0.1 fusion
  5.5 0.9 copy.24.masked
  6.3 0.7 and_select_fusion.refs_5_.refs_8_
  7.1 103.8 %enter.1 = (bf16[1024,1536]{1,0:T(8,128)(2,1)}, bf16[512,1024]{1,0:T(8,128)(2,1)}, bf16[1024,1024]{1,0:T(8,128)(2,1)}, bf16[4,512,1024]{2,1,0:T(8,128)(2,1)}, bf...) custom-call(bf16[4,512,256]{2,1,0:T(8,128)(2,1)} %bitcast.28, ...), custom_call_target="tpu_custom_call" | custom-call | flops 10000000000 | bytes 100000000 | tf_op jit(solution)/shard_map/enter/pallas_call | solution.py:909
  110.8 56.5 %time_forward.1 = (bf16[8,1024,256]{2,1,0:T(8,128)(2,1)}, bf16[16,128,768]{2,1,0:T(8,128)(2,1)}, bf16[16,128,256]{2,1,0:T(8,128)(2,1)}, f32[16,4,128]{2,1,0:T(4,...) custom-call(bf16[4,128,1024]{2,1,0:T(8,128)(2,1)} %bitcast.32, ...), custom_call_target="tpu_custom_call" | custom-call | flops 10000000000 | bytes 100000000 | tf_op jit(solution)/shard_map/time_forward/pallas_call | solution.py:1292
  167.4 63.4 %feed.1 = (bf16[2,4,256,512]{3,2,1,0:T(8,128)(2,1)}, bf16[2,4,256,512]{3,2,1,0:T(8,128)(2,1)}, f32[512,1024]{1,0:T(8,128)}, bf16[512,1024]{1,0:T(8,128)(2,1)}, b...) custom-call(f32[512,1024]{1,0:T(8,128)} %get-tuple-element.53.resid_hbm, f32[512,1024]{1,0:T(8,128)} %bitcast.31, ...), custom_call_target="tpu_custom_call" | custom-call | flops 25999998976 | bytes 100000000 | tf_op jit(solution)/shard_map/feed/pallas_call | solution.py:1545
  230.8 54.1 %time_back.1 = (f32[4,128,1024]{2,1,0:T(8,128)}, bf16[1024,1024]{1,0:T(8,128)(2,1)}, f32[256,512]{1,0:T(8,128)}, bf16[4,512,256]{2,1,0:T(8,128)(2,1)}) custom-call(bf16[4,128,1024]{2,1,0:T(8,128)(2,1)} %bitcast.33, bf16[512,1024]{1,0:T(8,128)(2,1)} %get-tuple-element.64.refs_1_, bf16[16,128,768]{2,1,0:T(8,128)(2,1)} %get-tuple-element.65.refs_2_, ...), custom_call_target="tpu_custom_call" | custom-call | flops 10000000000 | bytes 100000000 | tf_op jit(solution)/shard_map/time_back/pallas_call | solution.py:1292
  284.9 0.0 copy-start.1
  284.9 100.7 %leave.1 = (f32[3,128,256]{2,1,0:T(8,128)}, f32[256,128]{1,0:T(8,128)}, f32[128,1024]{1,0:T(8,128)}, f32[1024,128]{1,0:T(8,128)}, f32[3,128,256]{2,1,0:T(8,128)}...) custom-call(f32[512,1024]{1,0:T(8,128)} %bitcast.30, ...), custom_call_target="tpu_custom_call" | custom-call | flops 20000000000 | bytes 100000000 | tf_op jit(solution)/shard_map/leave/pallas_call | solution.py:2010
  385.6 0.0 copy-start
  385.6 0.0 copy-done.1
  385.6 1.0 copy.41
  386.6 1.0 copy-done
  387.5 0.0 copy-start.9
  387.5 0.0 copy-start.8
  387.5 0.0 copy-start.5
  387.5 0.0 copy-start.7
  387.6 0.0 copy-start.4
  387.6 0.0 copy-start.6
  387.6 1.3 copy.42
  388.9 0.0 copy-done.9
  388.9 0.6 copy.43
  389.5 0.0 copy-done.8
  389.5 0.6 copy.44
  390.1 0.0 copy-done.5
  390.1 0.7 copy.45
  390.8 0.0 copy-done.7
  390.8 0.7 copy.46
  391.5 0.0 copy-done.4
  391.5 0.7 copy.47
  392.2 0.0 copy-done.6
  392.2 0.7 copy.48
  392.9 0.0 copy-done.3
  392.9 0.8 copy.49
  393.7 0.0 copy-done.2
  393.7 0.8 copy.50
  (10 shorter events, 0.1 us)
Async XLA Ops:
  2.1 2.8 collective-permute-start
  284.9 100.7 %copy-start.1 = (bf16[4,512,256]{2,1,0:T(8,128)(2,1)S(1)}, bf16[4,512,256]{2,1,0:T(8,128)(2,1)}, u32[]{:S(2)}) copy-start(bf16[4,512,256]{2,1,0:T(8,128)(2,1)} %get-tuple-element.70) | copy-start | bytes 3145732
  385.6 2.0 copy-start
  387.5 1.4 copy-start.9
  387.5 1.9 copy-start.8
  387.5 2.5 copy-start.5
  387.5 3.3 copy-start.7
  387.6 3.9 copy-start.4
  387.6 4.7 %copy-start.6 = (f32[256,128]{1,0:T(8,128)S(1)}, f32[256,128]{1,0:T(8,128)}, u32[]{:S(2)}) copy-start(f32[256,128]{1,0:T(8,128)} %get-tuple-element.113) | copy-start | bytes 393220
  388.9 4.0 %copy-start.3 = (f32[128,1024]{1,0:T(8,128)S(1)}, f32[128,1024]{1,0:T(8,128)}, u32[]{:S(2)}) copy-start(f32[128,1024]{1,0:T(8,128)} %get-tuple-element.114) | copy-start | bytes 1572868
  388.9 4.8 %copy-start.2 = (f32[1024,128]{1,0:T(8,128)S(1)}, f32[1024,128]{1,0:T(8,128)}, u32[]{:S(2)}) copy-start(f32[1024,128]{1,0:T(8,128)} %get-tuple-element.115) | copy-start | bytes 1572868

commit v2 on v1

--- a/solution.py
+++ b/solution.py
@@ -937,10 +937,11 @@
 def time_kernel(back, scale, heads, *refs):
     if back:
         (own_ref, rider_ref, joined_hbm, total_ref, wide_ref, turned_ref, mixed_hbm, wt_hbm, bias_ref) = refs[:9]
-        (delta_ref, grad_ref, reduced_ref, rider_out) = refs[9:13]
-        (half_in, half_own, line_out, line_in, half_send, half_recv, half_local, line_send, line_recv) = refs[-17:-8]
-        (out_ref, turned, grad_qkv, grad_out, wt_ref, joined_ref, mixed_ref, load_sem) = refs[-8:]
-        refs = refs[13:-17]
+        (delta_ref, grad_hbm, reduced_ref, rider_out) = refs[9:13]
+        (half_in, half_own, line_out, line_in, half_send, half_recv, half_local, line_send, line_recv) = refs[-18:-9]
+        (out_ref, turned, grad_qkv, grad_out, wt_ref, joined_ref, mixed_ref, load_sem, grad_ref) = refs[-9:]
+        refs = refs[13:-18]
+        save_grad = pltpu.make_async_copy(grad_ref, grad_hbm, load_sem.at[0])
     else:
         (own_ref, rider_ref, far_ref, in_ref, wt_hbm, bias_ref) = refs[:6]
         (turned_ref, out_hbm, mixed_hbm, total_ref, delta_ref, rider_out, spread_out, in_out) = refs[6:14]
@@ -1223,6 +1224,7 @@
         grad_out[...] = jnp.zeros_like(grad_out)
         lax.fori_loop(0, chunks, weigh, 0)
         lax.fori_loop(0, grad_ref.shape[0] // BLK, arrange, 0)
+        save_grad.start()
     for k in range(chunks):
         scatter_y(k).wait_recv()
         delta_ref[:, patches(k)] = delta_ref[:, patches(k)] + near_in[k].astype(F32)
@@ -1234,6 +1236,7 @@
             line_away(r).wait_send()
         for s in range(4):
             half_away(s).wait_send()
+        save_grad.wait()
     for k in range(chunks):
         for copy in (gather_y(k), gather_c(k), gather_d(k), scatter_c(k), scatter_y(k)):
             copy.wait_send()
@@ -1294,7 +1297,7 @@
         in_specs=[anywhere] * 2
         + ([anywhere, whole, anywhere, anywhere, anywhere] if back else [anywhere] * 2)
         + [anywhere, whole],
-        out_specs=([] if back else [anywhere] * 3) + [whole] * (3 if back else 2) + [anywhere] * (held - 1),
+        out_specs=([] if back else [anywhere] * 3) + ([whole, anywhere, whole] if back else [whole] * 2) + [anywhere] * (held - 1),
         out_shape=out_shape,
         scratch_shapes=[
             pltpu.VMEM((features, 3 * width), BF16),
@@ -1319,7 +1322,7 @@
         + ([pltpu.VMEM(saved[0].shape, BF16), pltpu.VMEM(saved[4].shape, BF16)] if back else [])
         + ([] if back else [pltpu.VMEM(out_shape[1].shape, BF16), pltpu.VMEM(out_shape[2].shape, BF16)])
         + [dma((4,))]
-        + ([] if back else [dma((2, chunks))]),
+        + [pltpu.VMEM((features, features), BF16) if back else dma((2, chunks))],
         compiler_params=pltpu.CompilerParams(
             collective_id=2 if back else 1, has_side_effects=True, vmem_limit_bytes=60 * 1024 * 1024
         ),

time: 396 us -> 396 us (level)
  no operation moved by 1% of the time
where the time goes in v2:
time: 396 us; the launch traced here: 394 us
  Pallas kernels  378 us (95%)
  local copies, waits for them, and re-layouts  11.6 us (3%)
    pallas_call x2, Pallas kernels, time_call(): pl.pallas_call(functools.partial(time_kernel, back, scale, heads), in_spe...  110 us
    pallas_call x1, Pallas kernels, enter(): pl.pallas_call(functools.partial(enter_kernel, scale), in_specs=[anywhere...  104 us
    pallas_call x1, Pallas kernels, leave(): pl.pallas_call(functools.partial(leave_kernel, scale), in_specs=[anywhere...  101 us
    pallas_call x1, Pallas kernels, feed(): pl.pallas_call(feed_kernel, in_specs=[anywhere] * 3 + [whole] * 2 + [anyw...  63.4 us
    unnamed x31, local copies, waits for them, and re-layouts  8.86 us
  transfers between devices with their start and end apart: 1, of which 0 were waited for; matrix products, arithmetic and copies ran while one was open for 1% of the time, Pallas kernels for 0%

profile of v2, /device:TPU:9, one launch (start us, length us, event | category | flops | bytes accessed | tf_op | source)
XLA Modules:
  0.0 393.9 jit_solution(9576254327048454571)
XLA Ops:
  0.6 0.8 convert_bitcast_fusion
  1.4 0.7 constant_dynamic-update-slice_fusion
  2.1 0.7 collective-permute-start
  2.8 0.7 broadcast_in_dim.21
  3.4 0.1 pad.2.clone
  3.5 1.3 maximum_maximum_fusion.vec
  4.9 0.0 collective-permute-done
  4.9 0.1 dynamic-slice_reduce_fusion
  5.0 0.1 reshape.109
  5.1 0.1 reshape.110
  5.2 0.1 broadcast_in_dim.23
  5.3 0.1 le.15
  5.4 0.1 fusion
  5.5 0.9 copy.24.masked
  6.3 0.7 and_select_fusion.refs_5_.refs_8_
  7.1 103.8 %enter.1 = (bf16[1024,1536]{1,0:T(8,128)(2,1)}, bf16[512,1024]{1,0:T(8,128)(2,1)}, bf16[1024,1024]{1,0:T(8,128)(2,1)}, bf16[4,512,1024]{2,1,0:T(8,128)(2,1)}, bf...) custom-call(bf16[4,512,256]{2,1,0:T(8,128)(2,1)} %bitcast.28, ...), custom_call_target="tpu_custom_call" | custom-call | flops 10000000000 | bytes 100000000 | tf_op jit(solution)/shard_map/enter/pallas_call | solution.py:909
  110.8 56.5 %time_forward.1 = (bf16[8,1024,256]{2,1,0:T(8,128)(2,1)}, bf16[16,128,768]{2,1,0:T(8,128)(2,1)}, bf16[16,128,256]{2,1,0:T(8,128)(2,1)}, f32[16,4,128]{2,1,0:T(4,...) custom-call(bf16[4,128,1024]{2,1,0:T(8,128)(2,1)} %bitcast.32, ...), custom_call_target="tpu_custom_call" | custom-call | flops 10000000000 | bytes 100000000 | tf_op jit(solution)/shard_map/time_forward/pallas_call | solution.py:1295
  167.4 63.4 %feed.1 = (bf16[2,4,256,512]{3,2,1,0:T(8,128)(2,1)}, bf16[2,4,256,512]{3,2,1,0:T(8,128)(2,1)}, f32[512,1024]{1,0:T(8,128)}, bf16[512,1024]{1,0:T(8,128)(2,1)}, b...) custom-call(f32[512,1024]{1,0:T(8,128)} %get-tuple-element.53.resid_hbm, f32[512,1024]{1,0:T(8,128)} %bitcast.31, ...), custom_call_target="tpu_custom_call" | custom-call | flops 25999998976 | bytes 100000000 | tf_op jit(solution)/shard_map/feed/pallas_call | solution.py:1548
  230.8 53.4 %time_back.1 = (f32[4,128,1024]{2,1,0:T(8,128)}, bf16[1024,1024]{1,0:T(8,128)(2,1)}, f32[256,512]{1,0:T(8,128)}, bf16[4,512,256]{2,1,0:T(8,128)(2,1)}) custom-call(bf16[4,128,1024]{2,1,0:T(8,128)(2,1)} %bitcast.33, bf16[512,1024]{1,0:T(8,128)(2,1)} %get-tuple-element.64.refs_1_, bf16[16,128,768]{2,1,0:T(8,128)(2,1)} %get-tuple-element.65.refs_2_, ...), custom_call_target="tpu_custom_call" | custom-call | flops 10000000000 | bytes 100000000 | tf_op jit(solution)/shard_map/time_back/pallas_call | solution.py:1295
  284.2 0.0 copy-start.1
  284.3 100.7 %leave.1 = (f32[3,128,256]{2,1,0:T(8,128)}, f32[256,128]{1,0:T(8,128)}, f32[128,1024]{1,0:T(8,128)}, f32[1024,128]{1,0:T(8,128)}, f32[3,128,256]{2,1,0:T(8,128)}...) custom-call(f32[512,1024]{1,0:T(8,128)} %bitcast.30, ...), custom_call_target="tpu_custom_call" | custom-call | flops 20000000000 | bytes 100000000 | tf_op jit(solution)/shard_map/leave/pallas_call | solution.py:2013
  385.0 0.0 copy-start
  385.0 0.0 copy-done.1
  385.0 1.0 copy.41
  386.0 1.0 copy-done
  387.0 0.0 copy-start.9
  387.0 0.0 copy-start.8
  387.0 0.0 copy-start.5
  387.0 0.0 copy-start.7
  387.0 0.0 copy-start.4
  387.0 0.0 copy-start.6
  387.0 1.3 copy.42
  388.3 0.0 copy-done.9
  388.3 0.6 copy.43
  388.9 0.0 copy-done.8
  388.9 0.6 copy.44
  389.5 0.0 copy-done.5
  389.5 0.7 copy.45
  390.2 0.0 copy-done.7
  390.2 0.7 copy.46
  390.9 0.0 copy-done.4
  390.9 0.7 copy.47
  391.6 0.0 copy-done.6
  391.6 0.7 copy.48
  392.3 0.0 copy-done.3
  392.3 0.8 copy.49
  393.1 0.0 copy-done.2
  393.1 0.8 copy.50
  (10 shorter events, 0.1 us)
Async XLA Ops:
  2.1 2.8 collective-permute-start
  284.2 100.7 %copy-start.1 = (bf16[4,512,256]{2,1,0:T(8,128)(2,1)S(1)}, bf16[4,512,256]{2,1,0:T(8,128)(2,1)}, u32[]{:S(2)}) copy-start(bf16[4,512,256]{2,1,0:T(8,128)(2,1)} %get-tuple-element.70) | copy-start | bytes 3145732
  385.0 2.0 copy-start
  387.0 1.4 copy-start.9
  387.0 1.9 copy-start.8
  387.0 2.5 copy-start.5
  387.0 3.3 copy-start.7
  387.0 3.9 copy-start.4
  387.0 4.7 %copy-start.6 = (f32[256,128]{1,0:T(8,128)S(1)}, f32[256,128]{1,0:T(8,128)}, u32[]{:S(2)}) copy-start(f32[256,128]{1,0:T(8,128)} %get-tuple-element.113) | copy-start | bytes 393220
  388.3 4.0 %copy-start.3 = (f32[128,1024]{1,0:T(8,128)S(1)}, f32[128,1024]{1,0:T(8,128)}, u32[]{:S(2)}) copy-start(f32[128,1024]{1,0:T(8,128)} %get-tuple-element.114) | copy-start | bytes 1572868
  388.3 4.8 %copy-start.2 = (f32[1024,128]{1,0:T(8,128)S(1)}, f32[1024,128]{1,0:T(8,128)}, u32[]{:S(2)}) copy-start(f32[1024,128]{1,0:T(8,128)} %get-tuple-element.115) | copy-start | bytes 1572868
